TPU v7x, 128 devices: a whole 4x4x4 slice. The times are simulated.
128 devices in a mesh: dp: 4 (over z_hi, core), expert: 32 (over z_lo, y, x).
Axes of the slice: x: 4, y: 4, z: 4 (z_hi: 2, z_lo: 2; z = z_hi * 2 + z_lo), core: 2. Of those that a mesh axis runs over, the one named last changes fastest.
Arguments:
- queries: bfloat16 [1024, 4096], P(('dp', 'expert')), may hold values from -9 to 9
- kv_pool: bfloat16 [16384, 16, 1024], P(('dp', 'expert')), may hold values from -9 to 9
- page_table: int32 [1024, 4, 16], P(('dp', 'expert')), may hold values from 0 to 127
- held_tokens: int32 [1024, 4], P(('dp', 'expert')), may hold values from 1 to 256, as said below
- sinks: float32 [64], replicated, may hold values from 2 to 8
- residual: bfloat16 [1024, 2880], P(('dp', 'expert')), may hold values from -100 to 100
- route_ids: int32 [1024, 4], P(('dp', 'expert')), may hold values from 0 to 31, all different within a row; in each aligned block of 8 rows (0 to 7, 8 to 15, ...) at most 2 rows name the same one
- route_weights: float32 [1024, 4], P(('dp', 'expert')), may hold values from 0.1 to 1
- moe_gain: float32 [2880], replicated, may hold values from 0.25 to 1.75
- w_gate: bfloat16 [32, 2880, 1536], P('expert', None, 'dp')
- w_up: bfloat16 [32, 2880, 1536], P('expert', None, 'dp')
- w_down: bfloat16 [32, 1536, 2880], P('expert', 'dp'), may hold values from -0.078125 to 0.078125
- o_weight: bfloat16 [4096, 2880], P(None, 'dp'), may hold values from -0.09375 to 0.09375
- attn_gain: float32 [2880], replicated, may hold values from 0.25 to 1.75
- qkv_weight: bfloat16 [2880, 5120], P(None, 'dp'), may hold values from -0.109375 to 0.109375
Outputs:
- next_stream: bfloat16 [1024, 2880], P(('dp', 'expert'))
- next_qkv: bfloat16 [1024, 5120], P(('dp', 'expert'))
Inputs may be any that keep to these rules, and one draw needn't show every extreme that they name: `route_ids`: each row names 4 different experts; among the 8 rows of one device no expert is named more than 2 times, a bound that some block reaches. `page_table`: pages may be shared between requests. `held_tokens`: the largest value is reached in every draw.
All inputs are finite; a program needn't handle non-finite values.
Results may differ from a plain program's by a relative error of at most 0.0145.
Values may be sent and summed in bfloat16 or wider, within the bound.
A program may use at most 128 MiB of HBM per device.

v0:
```python
import math

import jax
import jax.numpy as jnp
from jax import lax
from jax.sharding import PartitionSpec as P

HEADS = 64
KVH = 8
HD = 64
TOP = 4
PAGE = 16
PPH = 16


EPSILON = 1e-05
LIMIT = 7.0


def rms_scale(values, gain):
    wide = values.astype(jnp.float32)
    scale = lax.rsqrt(jnp.mean(wide * wide, axis=-1, keepdims=True) + EPSILON)
    return (wide * scale * gain).astype(jnp.bfloat16)


def scale_heads(numerator, factor):
    return numerator * jnp.repeat(factor, HD, axis=1)


def head_tables():
    groups = HEADS // KVH
    columns = jnp.arange(KVH * HD, dtype=jnp.int32)
    head_group = jnp.arange(HEADS, dtype=jnp.int32) // groups
    head_mask = columns[None, :] // HD == head_group[:, None]
    fold_table = (columns[:, None] % HD == jnp.arange(HD, dtype=jnp.int32)[None, :]).astype(
        jnp.float32
    )
    return (head_mask, fold_table)


def holder_block(query_rows, page_rows, count_rows, kv_pool, head_mask, fold_table):
    blocks = query_rows.shape[0]
    token_span = PPH * PAGE
    width = KVH * HD
    fetched = kv_pool[page_rows].reshape(blocks, token_span, 2 * width)
    keys_part = fetched[:, :, :width]
    values_part = fetched[:, :, width:]
    query_heads = query_rows.reshape(blocks, HEADS, HD)
    spread = jnp.where(
        head_mask[None], jnp.tile(query_heads, (1, 1, KVH)), jnp.zeros((), jnp.bfloat16)
    )
    scores = jnp.einsum("bhe,ble->bhl", spread, keys_part, preferred_element_type=jnp.float32) * (
        1.0 / math.sqrt(HD)
    )
    usable = (jnp.arange(token_span, dtype=jnp.int32)[None, :] < count_rows[:, None])[:, None, :]
    highest = jnp.max(jnp.where(usable, scores, -1e30), axis=-1)
    weights = jnp.where(usable, jnp.exp(scores - highest[..., None]), 0.0)
    totals = jnp.sum(weights, axis=-1)
    every_value = jnp.einsum(
        "bhl,ble->bhe",
        weights.astype(jnp.bfloat16),
        values_part,
        preferred_element_type=jnp.float32,
    )
    own_value = jnp.where(head_mask[None], every_value, 0.0)
    numerator = jnp.einsum("bhe,ed->bhd", own_value, fold_table, precision=lax.Precision.HIGHEST)
    return (highest, totals, numerator.reshape(blocks, HEADS * HD))


def expert_apply(rows, gate_w, up_w, down_w):
    gate_proj = jnp.minimum(jnp.dot(rows, gate_w, preferred_element_type=jnp.float32), LIMIT)
    up_proj = jnp.clip(jnp.dot(rows, up_w, preferred_element_type=jnp.float32), -LIMIT, LIMIT)
    activated = (gate_proj * jax.nn.sigmoid(1.702 * gate_proj) * (up_proj + 1.0)).astype(
        jnp.bfloat16
    )
    return jnp.dot(activated, down_w, preferred_element_type=jnp.float32)


def body(
    queries,
    kv_pool,
    page_table,
    held_tokens,
    sinks,
    residual,
    route_ids,
    route_weights,
    moe_gain,
    w_gate,
    w_up,
    w_down,
    o_weight,
    attn_gain,
    qkv_weight,
):
    dp_count = lax.axis_size("dp")
    experts_count = lax.axis_size("expert")
    own_rows = queries.shape[0]
    tables, held_rows = (
        lax.all_gather(page_table, "dp", axis=0, tiled=True),
        lax.all_gather(held_tokens, "dp", axis=0, tiled=True),
    )
    group_queries = lax.all_gather(queries, "dp", axis=0, tiled=True)
    holder = lax.axis_index("dp")
    own_pages = lax.dynamic_index_in_dim(tables, holder, 1, keepdims=False)
    own_counts = lax.dynamic_index_in_dim(held_rows, holder, 1, keepdims=False)
    group_rows = group_queries.shape[0]
    block_rows = 32
    step_total = group_rows // block_rows
    head_mask, fold_table = head_tables()

    def run_block(items):
        return holder_block(items[0], items[1], items[2], kv_pool, head_mask, fold_table)

    highest, totals, numerator = lax.map(
        run_block,
        (
            group_queries.reshape(step_total, block_rows, HEADS * HD),
            own_pages.reshape(step_total, block_rows, PPH),
            own_counts.reshape(step_total, block_rows),
        ),
    )
    highest = highest.reshape(group_rows, HEADS)
    totals = totals.reshape(group_rows, HEADS)
    numerator = numerator.reshape(group_rows, HEADS * HD)
    peak_score = lax.pmax(highest, "dp")
    factor = jnp.exp(highest - peak_score)
    totals, numerator = (
        lax.psum((totals * factor).astype(jnp.bfloat16), "dp").astype(jnp.float32),
        lax.psum(scale_heads(numerator, factor).astype(jnp.bfloat16), "dp").astype(jnp.float32),
    )
    highest = peak_score
    ceiling = jnp.maximum(highest, sinks[None, :])
    kept = jnp.exp(highest - ceiling)
    denominator = totals * kept + jnp.exp(sinks[None, :] - ceiling)
    attention = scale_heads(numerator, kept / denominator).astype(jnp.bfloat16)
    projected = jnp.dot(attention, o_weight, preferred_element_type=jnp.float32).astype(
        jnp.bfloat16
    )
    attention_out = lax.all_to_all(projected, "dp", split_axis=0, concat_axis=1, tiled=True)
    stream = (residual.astype(jnp.float32) + attention_out.astype(jnp.float32)).astype(jnp.bfloat16)
    moe_input = rms_scale(stream, moe_gain)
    capacity = 2 * own_rows * TOP // experts_count
    chosen = (
        route_ids[:, :, None] == jnp.arange(experts_count, dtype=jnp.int32)[None, None, :]
    ).astype(jnp.int32)
    flat_chosen = chosen.reshape(own_rows * TOP, experts_count)
    before = jnp.cumsum(flat_chosen, axis=0) - flat_chosen
    slot_index = jnp.sum(before * flat_chosen, axis=1).reshape(own_rows, TOP)
    placed = chosen[:, :, :, None] * (
        slot_index[:, :, None, None] == jnp.arange(capacity, dtype=jnp.int32)[None, None, None, :]
    ).astype(jnp.int32)
    placed = placed.reshape(own_rows, TOP, experts_count * capacity)
    dispatch = jnp.sum(placed, axis=1).astype(jnp.bfloat16)
    route_share = route_weights / jnp.sum(route_weights, axis=1, keepdims=True)
    combine = jnp.einsum(
        "rk,rkc->rc", route_share, placed.astype(jnp.float32), precision=lax.Precision.HIGHEST
    )
    send_rows = jnp.einsum(
        "rc,rd->cd", dispatch, moe_input, preferred_element_type=jnp.float32
    ).astype(jnp.bfloat16)
    gate_local = w_gate[0]
    up_local = w_up[0]
    down_local = w_down[0]
    copies = jnp.broadcast_to(send_rows[None], (dp_count,) + send_rows.shape).reshape(
        dp_count * send_rows.shape[0], send_rows.shape[1]
    )
    arrived = lax.all_to_all(copies, ("dp", "expert"), split_axis=0, concat_axis=0, tiled=True)
    partial_value = expert_apply(arrived, gate_local, up_local, down_local)
    came_back = lax.all_to_all(
        partial_value.astype(jnp.bfloat16),
        ("dp", "expert"),
        split_axis=0,
        concat_axis=0,
        tiled=True,
    ).astype(partial_value.dtype)
    returned = jnp.sum(came_back.reshape(dp_count, send_rows.shape[0], send_rows.shape[1]), axis=0)
    moe_out = jnp.dot(
        combine, returned, precision=lax.Precision.HIGHEST, preferred_element_type=jnp.float32
    )
    next_stream = (stream.astype(jnp.float32) + moe_out).astype(jnp.bfloat16)
    qkv_input = rms_scale(next_stream, attn_gain)
    group_qkv = jnp.dot(
        lax.all_gather(qkv_input, "dp", axis=0, tiled=True),
        qkv_weight,
        preferred_element_type=jnp.float32,
    ).astype(jnp.bfloat16)
    next_qkv = lax.all_to_all(group_qkv, "dp", split_axis=0, concat_axis=1, tiled=True)
    return (next_stream, next_qkv)


def solution(mesh):
    in_specs = (
        P(("dp", "expert"), None),
        P(("dp", "expert"), None, None),
        P(("dp", "expert"), None, None),
        P(("dp", "expert"), None),
        P(),
        P(("dp", "expert"), None),
        P(("dp", "expert"), None),
        P(("dp", "expert"), None),
        P(),
        P("expert", None, "dp"),
        P("expert", None, "dp"),
        P("expert", "dp", None),
        P(None, "dp"),
        P(),
        P(None, "dp"),
    )
    out_specs = (P(("dp", "expert"), None), P(("dp", "expert"), None))
    return jax.shard_map(body, mesh=mesh, in_specs=in_specs, out_specs=out_specs, check_vma=False)
```

profile of v0, /device:TPU:1, one launch (start us, length us, event | category | flops | bytes accessed | tf_op | source)
XLA Modules:
  0.0 265.4 jit_solution(2009156426341383861)
XLA Ops:
  7.3 8.6 %all-gather = s32[4,8,4]{1,2,0:T(4,128)S(1)} all-gather(s32[1,8,4]{1,2,0:T(4,128)} %bitcast.60), channel_id=1, replica_groups=mesh['dp'=4,'expert'=32] {'dp'}, dimensions={0}, use_global_device_ids=true | all-gather | bytes 640 | tf_op jit(solution)/shard_map/all_gather | solution.py:101
  16.1 7.2 %all_gather.14 = s32[32,4,16]{2,1,0:T(4,128)S(1)} all-gather(s32[8,4,16]{2,1,0:T(4,128)} %param.17), channel_id=1, replica_groups=mesh['dp'=4,'expert'=32] {'dp'}, dimensions={0}, use_global_device_ids=true | all-gather | bytes 10240 | tf_op jit(solution)/shard_map/all_gather | solution.py:100
  23.4 7.7 %all_gather.13 = bf16[32,4096]{1,0:T(8,128)(2,1)S(1)} all-gather(bf16[8,4096]{1,0:T(8,128)(2,1)} %param.15), channel_id=1, replica_groups=mesh['dp'=4,'expert'=32] {'dp'}, dimensions={0}, use_global_device_ids=true | all-gather | bytes 327680 | tf_op jit(solution)/shard_map/all_gather | solution.py:103
  31.7 2.7 %tile.15 = bf16[32,64,8,64]{3,2,1,0:T(8,128)(2,1)} broadcast(bf16[32,64,64]{2,1,0:T(8,128)(2,1)S(1)} %tile.14), dimensions={0,1,3} | broadcast | bytes 2359296 | tf_op jit(solution)/shard_map/while/body/eval_jaxpr/tile | solution.py:50
  34.4 6.4 %tile.16 = bf16[32,64,512]{2,1,0:T(8,128)(2,1)} reshape(bf16[32,64,8,64]{3,2,1,0:T(8,128)(2,1)} %tile.15) | data formatting | bytes 4194304 | tf_op jit(solution)/shard_map/while/body/eval_jaxpr/tile | solution.py:50
  40.8 16.1 %gather_fusion = bf16[512,16,1024]{2,1,0:T(8,128)(2,1)} fusion(bf16[128,16,1024]{2,1,0:T(8,128)(2,1)} %param.16, s32[1024]{0:T(1024)S(1)} %pad_clamp_fusion), kind=kCustom, calls=%fused_computation | custom fusion | bytes 33556480 | tf_op jit(solution)/shard_map/while/body/eval_jaxpr/gather | solution.py:45
  57.0 8.0 %select_reduce_fusion = (f32[32,64]{1,0:T(8,128)S(1)}, f32[32,64,256]{2,1,0:T(8,128)}) fusion(pred[32,256]{1,0:T(8,128)(4,1)S(1)} %iota_compare_fusion.2, bf16[32,256,1024]{2,1,0:T(8,128)(2,1)} %bitcast.54, bf16[32,64,512]{2,1,0:T(8,128)(2,1)} %tile.16, pred[64,512]{1,0:T(8,128)(4,1)S(1)} %broadcast_compare_fusion), kind=kOutput, calls=%fused_computation.20 | convolution fusion | flops 539490304 | bytes 12632064 | tf_op jit(solution)/shard_map/while/body/eval_jaxpr/bhe,ble->bhl/dot_general | solution.py:52
  65.1 12.4 %pmax.7 = f32[32,64]{1,0:T(8,128)S(1)} all-reduce(f32[32,64]{1,0:T(8,128)S(1)} %get-tuple-element.28), channel_id=1, replica_groups=mesh['dp'=4,'expert'=32] {'dp'}, use_global_device_ids=true, to_apply=%region_1.2 | all-reduce | flops 2048 | bytes 16384 | tf_op jit(solution)/shard_map/pmax | solution.py:126
  77.5 2.5 fusion.17
  80.0 4.3 %fusion = f32[32,64,512]{2,1,0:T(8,128)S(1)} fusion(bf16[32,256,1024]{2,1,0:T(8,128)(2,1)} %bitcast.55, f32[32,64,256]{2,1,0:T(8,128)S(1)} %copy-done.1, f32[32,64]{1,0:T(8,128)S(1)} %get-tuple-element.28, pred[32,256]{1,0:T(8,128)(4,1)S(1)} %iota_compare_fusion.2), kind=kOutput, calls=%fused_computation.1 | convolution fusion | flops 538968064 | bytes 14696448 | tf_op jit(solution)/shard_map/while/body/eval_jaxpr/bhl,ble->bhe/dot_general | solution.py:59
  84.4 2.2 fusion.22
  86.6 1.2 convert_element_type.109
  87.8 10.5 %psum.15 = bf16[32,64]{1,0:T(8,128)(2,1)S(1)} all-reduce(bf16[32,64]{1,0:T(8,128)(2,1)S(1)} %get-tuple-element.24), channel_id=1, replica_groups=mesh['dp'=4,'expert'=32] {'dp'}, use_global_device_ids=true, to_apply=%region_4.5 | all-reduce | flops 2048 | bytes 8192 | tf_op jit(solution)/shard_map/psum | solution.py:129
  100.6 31.0 %all-reduce.2.cloned.1.call-done = bf16[32,4096]{1,0:T(8,128)(2,1)} async-done(((bf16[32,4096]{1,0:T(8,128)(2,1)}), bf16[32,4096]{1,0:T(8,128)(2,1)}) %all-reduce.2.cloned.1.call-update) | async-done | bytes 262160 | tf_op jit(solution)/shard_map/psum | solution.py:130
  131.5 5.3 %fusion.40 = bf16[4,8,720]{2,1,0:T(8,128)(2,1)} fusion(bf16[4096,720]{0,1:T(8,128)(2,1)} %param.27, f32[32,4096]{1,0:T(8,128)} %reshape.243, bf16[32,4096]{1,0:T(8,128)(2,1)} %all-reduce.2.cloned.1.call-done), kind=kOutput, calls=%fused_computation.34 | convolution fusion | flops 189159936 | bytes 6730752 | tf_op jit(solution)/shard_map/dot_general | solution.py:137
  136.9 3.4 %all-to-all-start = ((bf16[4,8,720]{2,1,0:T(8,128)(2,1)}), bf16[4,8,720]{2,1,0:T(8,128)(2,1)S(1)}, u32[]{:S(2)}, u32[]{:S(2)}) async-start(bf16[4,8,720]{2,1,0:T(8,128)(2,1)} %fusion.40), calls=%async_computation | async-start | bytes 98304 | tf_op jit(solution)/shard_map/all_to_all | solution.py:140
  140.4 4.6 %all-to-all-done = bf16[4,8,720]{2,1,0:T(8,128)(2,1)S(1)} async-done(((bf16[4,8,720]{2,1,0:T(8,128)(2,1)}), bf16[4,8,720]{2,1,0:T(8,128)(2,1)S(1)}, u32[]{:S(2)}, u32[]{:S(2)}) %all-to-all-start) | async-done | bytes 46112 | tf_op jit(solution)/shard_map/all_to_all | solution.py:140
  145.7 1.2 broadcast_in_dim.109
  146.9 4.3 %all_to_all.40 = bf16[128,2,2880]{2,1,0:T(2,128)(2,1)} reshape(bf16[4,64,2880]{2,1,0:T(8,128)(2,1)} %broadcast_in_dim.109) | data formatting | bytes 2949120 | tf_op jit(solution)/shard_map/all_to_all | solution.py:168
  151.2 30.7 %all_to_all.53 = bf16[128,2,2880]{2,1,0:T(2,128)(2,1)} all-to-all(bf16[128,2,2880]{2,1,0:T(2,128)(2,1)} %all_to_all.40), channel_id=1, replica_groups=mesh['dp'=4,'expert'=32] {'dp','expert'}, dimensions={0} | all-to-all | bytes 2949120 | tf_op jit(solution)/shard_map/all_to_all | solution.py:168
  181.9 4.4 %all_to_all.42 = bf16[256,2880]{1,0:T(8,128)(2,1)} reshape(bf16[128,2,2880]{2,1,0:T(2,128)(2,1)} %all_to_all.53) | data formatting | bytes 2949120 | tf_op jit(solution)/shard_map/all_to_all | solution.py:168
  186.3 3.0 %fusion.25 = f32[256,384]{1,0:T(8,128)S(1)} fusion(bf16[256,2880]{1,0:T(8,128)(2,1)} %all_to_all.42, bf16[1,2880,384]{2,1,0:T(8,128)(2,1)} %param.24), kind=kOutput, calls=%fused_computation.28 | convolution fusion | flops 566329344 | bytes 4079616 | tf_op jit(solution)/shard_map/dot_general | solution.py:71
  189.3 5.1 %convolution_convert_fusion = bf16[256,2880]{0,1:T(8,128)(2,1)} fusion(bf16[1,384,2880]{1,2,0:T(8,128)(2,1)S(1)} %copy-done, bf16[256,2880]{1,0:T(8,128)(2,1)} %all_to_all.42, bf16[1,2880,384]{2,1,0:T(8,128)(2,1)} %param.25, f32[256,384]{1,0:T(8,128)S(1)} %fusion.25), kind=kOutput, calls=%fused_computation.7 | convolution fusion | flops 1134084096 | bytes 7766016 | tf_op jit(solution)/shard_map/dot_general | solution.py:76
  194.4 2.6 copy.30
  197.0 4.3 %all_to_all.43 = bf16[128,2,2880]{2,1,0:T(2,128)(2,1)} reshape(bf16[256,2880]{1,0:T(8,128)(2,1)} %copy.30) | data formatting | bytes 2949120 | tf_op jit(solution)/shard_map/all_to_all | solution.py:170
  201.3 6.1 %all-to-all-start.2 = ((bf16[128,2,2880]{2,1,0:T(2,128)(2,1)}), bf16[128,2,2880]{2,1,0:T(2,128)(2,1)}, u32[]{:S(2)}, u32[]{:S(2)}) async-start(bf16[128,2,2880]{2,1,0:T(2,128)(2,1)} %all_to_all.43), calls=%async_computation.2 | async-start | bytes 3014656 | tf_op jit(solution)/shard_map/all_to_all | solution.py:170
  207.4 23.1 %all-to-all-done.2 = bf16[128,2,2880]{2,1,0:T(2,128)(2,1)} async-done(((bf16[128,2,2880]{2,1,0:T(2,128)(2,1)}), bf16[128,2,2880]{2,1,0:T(2,128)(2,1)}, u32[]{:S(2)}, u32[]{:S(2)}) %all-to-all-start.2) | async-done | bytes 1474592 | tf_op jit(solution)/shard_map/all_to_all | solution.py:170
  230.5 4.5 %reshape.245 = f32[4,64,2880]{2,1,0:T(8,128)} reshape(bf16[128,2,2880]{2,1,0:T(2,128)(2,1)} %all-to-all-done.2) | data formatting | bytes 4423680 | tf_op jit(solution)/shard_map/convert_element_type | solution.py:176
  235.1 2.1 reduce_sum.69
  237.9 8.4 %all_gather.15 = bf16[32,2880]{1,0:T(8,128)(2,1)S(1)} all-gather(bf16[8,2880]{1,0:T(8,128)(2,1)S(1)} %fusion.63), channel_id=1, replica_groups=mesh['dp'=4,'expert'=32] {'dp'}, dimensions={0}, use_global_device_ids=true | all-gather | bytes 230400 | tf_op jit(solution)/shard_map/all_gather | solution.py:184
  246.3 4.3 %fusion.7 = bf16[4,8,1280]{2,1,0:T(8,128)(2,1)S(1)} fusion(bf16[32,2880]{1,0:T(8,128)(2,1)S(1)} %all_gather.15, bf16[2880,1280]{1,0:T(8,128)(2,1)} %param.29), kind=kOutput, calls=%fused_computation.12 | convolution fusion | flops 235970560 | bytes 7639040 | tf_op jit(solution)/shard_map/dot_general | solution.py:183
  250.6 7.3 %all_to_all.54 = bf16[4,8,1280]{2,1,0:T(8,128)(2,1)S(1)} all-to-all(bf16[4,8,1280]{2,1,0:T(8,128)(2,1)S(1)} %fusion.7), channel_id=1, replica_groups=mesh['dp'=4,'expert'=32] {'dp'}, dimensions={0} | all-to-all | bytes 163840 | tf_op jit(solution)/shard_map/all_to_all | solution.py:188
  (61 shorter events, 5.3 us)
Async XLA Ops:
  7.2 182.2 %copy-start = (bf16[1,384,2880]{1,2,0:T(8,128)(2,1)S(1)}, bf16[1,384,2880]{1,2,0:T(8,128)(2,1)}, u32[]{:S(2)}) copy-start(bf16[1,384,2880]{1,2,0:T(8,128)(2,1)} %param.26) | copy-start | bytes 6635524
  7.2 124.4 %all-reduce.2.cloned.1.call-start = ((), (), s32[]{:S(2)}) async-start(), calls=%async_computation.4 | async-start | bytes 524288 | tf_op jit(solution)/shard_map/psum | solution.py:130
  77.5 2.5 copy-start.1
  84.4 14.0 %copy-start.6 = (s32[8,4]{0,1:T(4,128)S(1)}, s32[8,4]{0,1:T(4,128)}, u32[]{:S(2)}) copy-start(s32[8,4]{0,1:T(4,128)} %param.21) | copy-start | bytes 388
  84.4 14.6 %copy-start.8 = (f32[64]{0:T(128)S(1)}, f32[64]{0:T(128)}, u32[]{:S(2)}) copy-start(f32[64]{0:T(128)} %param.19) | copy-start | bytes 772
  100.6 44.6 %copy-start.3 = (bf16[8,2880]{1,0:T(8,128)(2,1)S(1)}, bf16[8,2880]{1,0:T(8,128)(2,1)}, u32[]{:S(2)}) copy-start(bf16[8,2880]{1,0:T(8,128)(2,1)} %param.20) | copy-start | bytes 138244
  100.6 44.8 %copy-start.5 = (f32[2880]{0:T(1024)S(1)}, f32[2880]{0:T(1024)}, u32[]{:S(2)}) copy-start(f32[2880]{0:T(1024)} %param.23) | copy-start | bytes 34564
  136.9 8.1 %all-to-all-start = ((bf16[4,8,720]{2,1,0:T(8,128)(2,1)}), bf16[4,8,720]{2,1,0:T(8,128)(2,1)S(1)}, u32[]{:S(2)}, u32[]{:S(2)}) async-start(bf16[4,8,720]{2,1,0:T(8,128)(2,1)} %fusion.40), calls=%async_computation | async-start | bytes 98304 | tf_op jit(solution)/shard_map/all_to_all | solution.py:140
  201.3 6.1 %copy-start.7 = (f32[8,4]{0,1:T(4,128)S(1)}, f32[8,4]{0,1:T(4,128)}, u32[]{:S(2)}) copy-start(f32[8,4]{0,1:T(4,128)} %param.22) | copy-start | bytes 388
  201.3 29.3 %all-to-all-start.2 = ((bf16[128,2,2880]{2,1,0:T(2,128)(2,1)}), bf16[128,2,2880]{2,1,0:T(2,128)(2,1)}, u32[]{:S(2)}, u32[]{:S(2)}) async-start(bf16[128,2,2880]{2,1,0:T(2,128)(2,1)} %all_to_all.43), calls=%async_computation.2 | async-start | bytes 3014656 | tf_op jit(solution)/shard_map/all_to_all | solution.py:170
  235.1 2.7 %copy-start.4 = (f32[2880]{0:T(1024)S(1)}, f32[2880]{0:T(1024)}, u32[]{:S(2)}) copy-start(f32[2880]{0:T(1024)} %param.28) | copy-start | bytes 34564
  237.8 12.8 %copy-start.2 = (bf16[8,2880]{1,0:T(8,128)(2,1)}, bf16[8,2880]{1,0:T(8,128)(2,1)S(1)}, u32[]{:S(2)}) copy-start(bf16[8,2880]{1,0:T(8,128)(2,1)S(1)} %get-tuple-element.44) | copy-start | bytes 138244
Sparse Core Ops, SparseCore 0:
  87.9 43.5 all-reduce.1
where the time goes:
time: 266 us; the launch traced here: 265 us
  blocking collectives  93 us (35%)
  waiting for transfers between devices  58.7 us (22%)
  local copies, waits for them, and re-layouts  51.1 us (19%)
  matrix products  33.2 us (12%)
  between operations  14.3 us (5%)
  starting transfers between devices  9.51 us (4%)
  other arithmetic  5.52 us (2%)
    psum x1, waiting for transfers between devices, body(): lax.psum(scale_heads(numerator, factor).astype(jnp.bfloat16), 'dp')  31 us
    all_to_all x1, blocking collectives, body(): lax.all_to_all(copies, ('dp', 'expert'), split_axis=0, concat_axis=0, til...  30.7 us
    all_to_all x1, waiting for transfers between devices, body(): lax.all_to_all(partial_value.astype(jnp.bfloat16), ('dp', 'expert'), spli...  23.1 us
    gather x1, local copies, waits for them, and re-layouts, holder_block(): fetched = kv_pool[page_rows].reshape(blocks, token_span, 2 * width)  16.1 us
    pmax x1, blocking collectives, body(): peak_score = lax.pmax(highest, 'dp')  12.4 us
    psum x1, blocking collectives, body(): lax.psum((totals * factor).astype(jnp.bfloat16), 'dp').astype(jnp.float32)  10.5 us
    another operation x3, local copies, waits for them, and re-layouts, holder_block(): jnp.tile(query_heads, (1, 1, KVH))  9.71 us
    all_to_all x2, local copies, waits for them, and re-layouts, body(): lax.all_to_all(copies, ('dp', 'expert'), split_axis=0, concat_axis=0, til...  8.73 us
  transfers between devices with their start and end apart: 3, of which 3 were waited for; matrix products, arithmetic and copies ran while one was open for 1% of the time, Pallas kernels for 0%

commit v1 on v0

v1 whole, which is shorter than its diff:
```python
import math

import jax
import jax.numpy as jnp
from jax import lax
from jax.experimental import pallas as pl
from jax.experimental.pallas import tpu as pltpu
from jax.sharding import PartitionSpec as P

HEADS = 64
KVH = 8
HD = 64
TOP = 4
PAGE = 16
PPH = 16
SPAN = PPH * PAGE
WIDE = KVH * HD
PAIR = 2 * HD
ROWS = 8
NDP = 4

EPSILON = 1e-05
LIMIT = 7.0
MESH = pl.DeviceIdType.MESH
F32 = jnp.float32
BF16 = jnp.bfloat16

S_TAB, S_Q, S_RES, S_COM, S_PAIR_N, S_PAIR_ML, S_X_N, S_X_ML, S_LHS, S_PROJ = 0, 3, 6, 9, 12, 14, 16, 18, 19, 20
N_SEM_A = 23


def rms_scale(values, gain):
    wide = values.astype(jnp.float32)
    scale = lax.rsqrt(jnp.mean(wide * wide, axis=-1, keepdims=True) + EPSILON)
    return (wide * scale * gain).astype(jnp.bfloat16)


def position():
    dp = lax.axis_index("dp")
    expert = lax.axis_index("expert")
    return dp, lax.div(dp, 2), lax.rem(dp, 2), expert


def group_peer(z, c, offset):
    return lax.rem(z + offset // 2, 2) * 2 + lax.rem(c + offset % 2, 2)


def remote(src, dst, sems, sent, landed, device):
    return pltpu.make_async_remote_copy(
        src_ref=src,
        dst_ref=dst,
        send_sem=sems[0].at[sent],
        recv_sem=sems[1].at[landed],
        device_id=device,
        device_id_type=MESH,
    )


def spread_queries(query):
    wide = query.astype(F32)
    turned = pltpu.roll(wide, HD, 1)
    row = lax.broadcasted_iota(jnp.int32, (HEADS // 2, PAIR), 0)
    lane = lax.broadcasted_iota(jnp.int32, (HEADS // 2, PAIR), 1)
    odd_group = lax.rem(lax.div(row, 4), 2) == 1
    own_half = (lane >= HD) == odd_group
    even = jnp.where(own_half, jnp.where(odd_group, turned, wide), 0.0)
    odd = jnp.where(own_half, jnp.where(odd_group, wide, turned), 0.0)
    tile = lax.div(row, 8)
    parts = []
    for heads in (even, odd):
        parts.append(jnp.concatenate([jnp.where(tile == t, heads, 0.0) for t in range(4)], axis=1))
    return jnp.concatenate(parts, axis=0).astype(BF16)


def fold_values(wide):
    row = lax.broadcasted_iota(jnp.int32, (HEADS // 2, PAIR), 0)
    lane = lax.broadcasted_iota(jnp.int32, (HEADS // 2, PAIR), 1)
    odd_group = lax.rem(lax.div(row, 4), 2) == 1

    def own_tiles(base):
        return jnp.concatenate(
            [wide[base + 8 * t : base + 8 * t + 8, PAIR * t : PAIR * t + PAIR] for t in range(4)], axis=0
        )

    even, odd = own_tiles(0), own_tiles(HEADS // 2)
    even = jnp.where(odd_group, pltpu.roll(even, HD, 1), even)
    odd = jnp.where(odd_group, odd, pltpu.roll(odd, HD, 1))
    return jnp.where(lane < HD, even, odd)


def pair_columns(column):
    lane = lax.broadcasted_iota(jnp.int32, (HEADS // 2, PAIR), 1)
    return jnp.where(lane < HD, column[: HEADS // 2], column[HEADS // 2 :])


def attend(queries, tables, pool, rows, write):
    token = lax.broadcasted_iota(jnp.int32, (HEADS, SPAN), 1)
    scores, held = [], []
    for row in rows:
        keys = jnp.concatenate([pool[tables[row, page], :, :WIDE] for page in range(PPH)], axis=0)
        spread = spread_queries(queries[row])
        scores.append(
            lax.dot_general(spread, keys, (((1,), (1,)), ((), ())), preferred_element_type=F32)
            * (1.0 / math.sqrt(HD))
        )
        held.append(token < tables[row, PPH])
    weights, highs, sums = [], [], []
    for score, usable in zip(scores, held):
        high = jnp.max(jnp.where(usable, score, -1e30), axis=1, keepdims=True)
        weight = jnp.where(usable, jnp.exp(score - high), 0.0)
        highs.append(high)
        sums.append(jnp.sum(weight, axis=1, keepdims=True))
        weights.append(weight.astype(BF16))
    results = []
    for row, weight in zip(rows, weights):
        values = jnp.concatenate([pool[tables[row, page], :, WIDE:] for page in range(PPH)], axis=0)
        results.append(fold_values(jnp.dot(weight, values, preferred_element_type=F32)))
    for row, result, high, total in zip(rows, results, highs, sums):
        write(row, result, high, total)


STEP = 4


def attention_kernel(
    q_ref, tab_ref, sink_ref, res_ref, com_ref, pool_hbm, ow_hbm,
    stream_ref, com_out,
    pool, ow, qall, tabv, tabs, resall, comall, keep_n, keep_ml, send_n, send_ml, recv_n, recv_ml,
    xs_n, xs_ml, xr_n, xr_ml, att, lhs, pall, load_sem, tab_sem, send_sem, recv_sem,
):
    dp, z, c, expert = position()
    sems = (send_sem, recv_sem)
    loads = [pltpu.make_async_copy(pool_hbm, pool, load_sem.at[0]), pltpu.make_async_copy(ow_hbm, ow, load_sem.at[1])]
    for load in loads:
        load.start()

    barrier = pltpu.get_barrier_semaphore()
    for offset in (1, 2, 3):
        pl.semaphore_signal(barrier, inc=1, device_id=(group_peer(z, c, offset), expert), device_id_type=MESH)
    own_tab = pltpu.make_async_copy(tab_ref.at[dp], tabs.at[dp], tab_sem.at[0])
    own_tab.start()
    block = c * 2 + z
    qall[dp] = q_ref[...]
    resall[block] = res_ref[...]
    comall[block] = com_ref[...]
    pl.semaphore_wait(barrier, 3)

    sent = []

    def send(src, dst, number, landed, offset):
        copy = remote(src, dst, sems, number, landed, (group_peer(z, c, offset), expert))
        copy.start()
        sent.append(copy)
        return copy

    tab_in, q_in, res_in, com_in = {}, {}, {}, {}
    for offset in (2, 3, 1):
        peer = group_peer(z, c, offset)
        tab_in[offset] = send(tab_ref.at[peer], tabv.at[dp], S_TAB + offset - 1, S_TAB + offset - 1, offset)
        q_in[offset] = send(q_ref, qall.at[dp], S_Q + offset - 1, S_Q + offset - 1, offset)
    for offset in (2, 3, 1):
        res_in[offset] = send(res_ref, resall.at[block], S_RES + offset - 1, S_RES + offset - 1, offset)
        com_in[offset] = send(com_ref, comall.at[block], S_COM + offset - 1, S_COM + offset - 1, offset)

    lane = lax.broadcasted_iota(jnp.int32, (HEADS, PAIR), 1)

    def run_block(offset, number, numerators, stats):
        at = group_peer(z, c, offset)
        half = z if number == 0 else 1 - z
        stats[number] = jnp.zeros((HEADS, PAIR), F32)

        def write(row, result, high, total):
            numerators[number, row] = result.astype(numerators.dtype)
            place = half * ROWS + row
            tile = jnp.where(lane == place, high, stats[number])
            stats[number] = jnp.where(lane == place + HD, total, tile)

        def step(index, carry):
            rows = [index * STEP + i for i in range(STEP)]
            attend(qall.at[at], tabs.at[at], pool, rows, write)
            return carry

        lax.fori_loop(0, ROWS // STEP, step, 0)

    def fetch_block(offset):
        at = group_peer(z, c, offset)
        tab_in[offset].wait_recv()
        copy = pltpu.make_async_copy(tabv.at[at], tabs.at[at], tab_sem.at[offset])
        copy.start()
        q_in[offset].wait_recv()
        copy.wait()

    def send_pair(number):
        return (
            send(send_n.at[number], recv_n.at[number], S_PAIR_N + number, S_PAIR_N + number, 1),
            send(send_ml.at[number], recv_ml.at[number], S_PAIR_ML + number, S_PAIR_ML + number, 1),
        )

    def factors(tile, number):
        half = z if number == 0 else 1 - z
        return pltpu.roll(tile, lax.rem(PAIR - half * ROWS, PAIR), 1)

    def merge_pair(number, incoming):
        for copy in incoming:
            copy.wait_recv()
        mine, other = keep_ml[number], recv_ml[number]
        high = jnp.maximum(mine, other)
        left, right = jnp.exp(mine - high), jnp.exp(other - high)
        total = mine * pltpu.roll(left, HD, 1) + other * pltpu.roll(right, HD, 1)
        keep_ml[number] = jnp.where(lane < HD, high, total)
        left, right = factors(left, number), factors(right, number)
        for row in range(ROWS):
            merged = keep_n[number, row] * pair_columns(left[:, row : row + 1]) + recv_n[number, row].astype(
                F32
            ) * pair_columns(right[:, row : row + 1])
            keep_n[number, row] = merged
            xs_n[number, row] = merged.astype(BF16)
        return send(xs_n.at[number], xr_n.at[1 - number], S_X_N + number, S_X_N + 1 - number, 2)

    own_tab.wait()
    loads[0].wait()
    run_block(0, 0, keep_n, keep_ml)
    fetch_block(1)
    run_block(1, 0, send_n, send_ml)
    pair_in = [send_pair(0)]
    fetch_block(3)
    run_block(3, 1, send_n, send_ml)
    pair_in.append(send_pair(1))
    cross_in = [merge_pair(0, pair_in[0])]
    fetch_block(2)
    run_block(2, 1, keep_n, keep_ml)
    cross_in.append(merge_pair(1, pair_in[1]))
    xs_ml[...] = keep_ml[0] + keep_ml[1]
    cross_ml = send(xs_ml, xr_ml, S_X_ML, S_X_ML, 2)

    cross_ml.wait_recv()
    mine, other, sink = xs_ml[...], xr_ml[...], sink_ref[...]
    top = jnp.maximum(jnp.maximum(mine, other), sink)
    left, right = jnp.exp(mine - top), jnp.exp(other - top)
    total = mine * pltpu.roll(left, HD, 1) + other * pltpu.roll(right, HD, 1)
    below = pltpu.roll(total, HD, 1) + jnp.exp(sink - top)
    left, right = left / below, right / below
    for number in (0, 1):
        cross_in[1 - number].wait_recv()
        one, two = factors(left, number), factors(right, number)
        half = z if number == 0 else 1 - z
        for row in range(ROWS):
            attention = keep_n[number, row] * pair_columns(one[:, row : row + 1]) + xr_n[number, row].astype(
                F32
            ) * pair_columns(two[:, row : row + 1])
            start = pl.multiple_of((half * ROWS + row) * (HEADS // 2), HEADS // 2)
            att[pl.ds(start, HEADS // 2), :] = attention
    for pair in range(HEADS // 2):
        lhs[c, :, PAIR * pair : PAIR * pair + PAIR] = att[pl.ds(pair, 2 * ROWS, stride=HEADS // 2), :].astype(BF16)
    lhs_in = send(lhs.at[c], lhs.at[c], S_LHS, S_LHS, 1)
    loads[1].wait()
    lhs_in.wait_recv()
    rows = jnp.concatenate([lhs[0], lhs[1]], axis=0)
    projected = lax.dot_general(rows, ow[...], (((1,), (1,)), ((), ())), preferred_element_type=F32)
    pall[dp] = projected.astype(BF16)
    proj_in = [
        send(pall.at[dp], pall.at[dp], S_PROJ + offset - 1, S_PROJ + offset - 1, offset) for offset in (2, 3, 1)
    ]
    for offset in (1, 2, 3):
        res_in[offset].wait_recv()
        com_in[offset].wait_recv()
    com_out[...] = comall[...]
    for copy in proj_in:
        copy.wait_recv()
    for k in range(NDP):
        residual = jnp.concatenate([resall[d, k].astype(F32) for d in range(NDP)], axis=0)
        stream_ref[k] = (residual + pall[k].astype(F32)).astype(BF16)
    for copy in sent:
        copy.wait_send()


def head_order(values):
    return values.reshape(HEADS // 2, 2).T.reshape(HEADS, 1)


def attention_call(queries, kv_pool, page_table, held_tokens, sinks, residual, combine, o_weight):
    width = residual.shape[1] // NDP
    q_pairs = queries.reshape(ROWS, HEADS // 2, PAIR)
    table = jnp.concatenate([page_table, held_tokens[:, :, None]], axis=2).transpose(1, 0, 2)
    table = jnp.pad(table, ((0, 0), (0, 0), (0, 128 - PPH - 1)))
    sink_tile = jnp.broadcast_to(head_order(sinks), (HEADS, PAIR))
    residual_blocks = residual.reshape(ROWS, NDP, width).transpose(1, 0, 2)
    vmem = pl.BlockSpec(memory_space=pltpu.VMEM)
    hbm = pl.BlockSpec(memory_space=pl.ANY)
    slots = combine.shape[1]
    return pl.pallas_call(
        attention_kernel,
        out_shape=(
            jax.ShapeDtypeStruct((NDP, NDP * ROWS, width), BF16),
            jax.ShapeDtypeStruct((NDP, ROWS, slots), F32),
        ),
        in_specs=[vmem] * 5 + [hbm] * 2,
        out_specs=(vmem, vmem),
        scratch_shapes=[
            pltpu.VMEM(kv_pool.shape, BF16),
            pltpu.VMEM((width, HEADS * HD), BF16),
            pltpu.VMEM((NDP, ROWS, HEADS // 2, PAIR), BF16),
            pltpu.VMEM((NDP, ROWS, 128), jnp.int32),
            pltpu.SMEM((NDP, ROWS, 128), jnp.int32),
            pltpu.VMEM((NDP, NDP, ROWS, width), BF16),
            pltpu.VMEM((NDP, ROWS, slots), F32),
            pltpu.VMEM((2, ROWS, HEADS // 2, PAIR), F32),
            pltpu.VMEM((2, HEADS, PAIR), F32),
            pltpu.VMEM((2, ROWS, HEADS // 2, PAIR), BF16),
            pltpu.VMEM((2, HEADS, PAIR), F32),
            pltpu.VMEM((2, ROWS, HEADS // 2, PAIR), BF16),
            pltpu.VMEM((2, HEADS, PAIR), F32),
            pltpu.VMEM((2, ROWS, HEADS // 2, PAIR), BF16),
            pltpu.VMEM((HEADS, PAIR), F32),
            pltpu.VMEM((2, ROWS, HEADS // 2, PAIR), BF16),
            pltpu.VMEM((HEADS, PAIR), F32),
            pltpu.VMEM((2 * ROWS * HEADS // 2, PAIR), F32),
            pltpu.VMEM((2, 2 * ROWS, HEADS * HD), BF16),
            pltpu.VMEM((NDP, NDP * ROWS, width), BF16),
            pltpu.SemaphoreType.DMA((2,)),
            pltpu.SemaphoreType.DMA((4,)),
            pltpu.SemaphoreType.DMA((N_SEM_A,)),
            pltpu.SemaphoreType.DMA((N_SEM_A,)),
        ],
        compiler_params=pltpu.CompilerParams(collective_id=0, has_side_effects=True, vmem_limit_bytes=50 * 2**20),
        name="attention",
    )(q_pairs, table, sink_tile, residual_blocks, combine, kv_pool, o_weight.T)


def expert_apply(rows, gate_w, up_w, down_w):
    gate_proj = jnp.minimum(jnp.dot(rows, gate_w, preferred_element_type=jnp.float32), LIMIT)
    up_proj = jnp.clip(jnp.dot(rows, up_w, preferred_element_type=jnp.float32), -LIMIT, LIMIT)
    activated = (gate_proj * jax.nn.sigmoid(1.702 * gate_proj) * (up_proj + 1.0)).astype(
        jnp.bfloat16
    )
    return jnp.dot(activated, down_w, preferred_element_type=jnp.float32)


def combine_table(route_ids, route_weights, experts_count, capacity, block):
    rows = route_ids.shape[0]
    experts = jnp.arange(experts_count, dtype=jnp.int32)
    chosen = route_ids[:, :, None] == experts[None, None, :]
    share = route_weights / jnp.sum(route_weights, axis=1, keepdims=True)
    shares = jnp.sum(jnp.where(chosen, share[:, :, None], 0.0), axis=1)
    hit = jnp.any(chosen, axis=1)
    earlier = jnp.arange(rows)[:, None] > jnp.arange(rows)[None, :]
    slot = jnp.sum(jnp.where(earlier[:, :, None] & hit[None, :, :], 1, 0), axis=1)
    column = jnp.arange(NDP * capacity, dtype=jnp.int32)[None, None, :]
    table = jnp.where(hit[:, :, None] & (column == (block * capacity + slot)[:, :, None]), shares[:, :, None], 0.0)
    return table.reshape(rows, experts_count * NDP * capacity)


def body(
    queries,
    kv_pool,
    page_table,
    held_tokens,
    sinks,
    residual,
    route_ids,
    route_weights,
    moe_gain,
    w_gate,
    w_up,
    w_down,
    o_weight,
    attn_gain,
    qkv_weight,
):
    dp_count = lax.axis_size("dp")
    experts_count = lax.axis_size("expert")
    own_rows = queries.shape[0]
    holder = lax.axis_index("dp")
    block = lax.rem(holder, 2) * 2 + lax.div(holder, 2)
    capacity = 2 * own_rows * TOP // experts_count
    table = combine_table(route_ids, route_weights, experts_count, capacity, block)
    streams, tables = attention_call(
        queries, kv_pool, page_table, held_tokens, sinks, residual, table, o_weight
    )
    stream = lax.dynamic_slice_in_dim(streams, block * own_rows, own_rows, 1)
    stream = stream.transpose(1, 0, 2).reshape(own_rows, -1)
    moe_input = rms_scale(stream, moe_gain)
    own = lax.dynamic_index_in_dim(tables, block, 0, keepdims=False)
    own = own.reshape(own_rows, experts_count, NDP, capacity)
    combine = jnp.sum(own, axis=2).reshape(own_rows, experts_count * capacity)
    dispatch = (combine > 0).astype(jnp.bfloat16)
    send_rows = jnp.einsum(
        "rc,rd->cd", dispatch, moe_input, preferred_element_type=jnp.float32
    ).astype(jnp.bfloat16)
    gate_local = w_gate[0]
    up_local = w_up[0]
    down_local = w_down[0]
    copies = jnp.broadcast_to(send_rows[None], (dp_count,) + send_rows.shape).reshape(
        dp_count * send_rows.shape[0], send_rows.shape[1]
    )
    arrived = lax.all_to_all(copies, ("dp", "expert"), split_axis=0, concat_axis=0, tiled=True)
    partial_value = expert_apply(arrived, gate_local, up_local, down_local)
    came_back = lax.all_to_all(
        partial_value.astype(jnp.bfloat16),
        ("dp", "expert"),
        split_axis=0,
        concat_axis=0,
        tiled=True,
    ).astype(partial_value.dtype)
    returned = jnp.sum(came_back.reshape(dp_count, send_rows.shape[0], send_rows.shape[1]), axis=0)
    moe_out = jnp.dot(
        combine, returned, precision=lax.Precision.HIGHEST, preferred_element_type=jnp.float32
    )
    next_stream = (stream.astype(jnp.float32) + moe_out).astype(jnp.bfloat16)
    qkv_input = rms_scale(next_stream, attn_gain)
    group_qkv = jnp.dot(
        lax.all_gather(qkv_input, "dp", axis=0, tiled=True),
        qkv_weight,
        preferred_element_type=jnp.float32,
    ).astype(jnp.bfloat16)
    next_qkv = lax.all_to_all(group_qkv, "dp", split_axis=0, concat_axis=1, tiled=True)
    return (next_stream, next_qkv)


def solution(mesh):
    in_specs = (
        P(("dp", "expert"), None),
        P(("dp", "expert"), None, None),
        P(("dp", "expert"), None, None),
        P(("dp", "expert"), None),
        P(),
        P(("dp", "expert"), None),
        P(("dp", "expert"), None),
        P(("dp", "expert"), None),
        P(),
        P("expert", None, "dp"),
        P("expert", None, "dp"),
        P("expert", "dp", None),
        P(None, "dp"),
        P(),
        P(None, "dp"),
    )
    out_specs = (P(("dp", "expert"), None), P(("dp", "expert"), None))
    return jax.shard_map(body, mesh=mesh, in_specs=in_specs, out_specs=out_specs, check_vma=False)
```

time: 266 us -> 154 us (0.58)
  blocking collectives: 93 us -> 49 us
  waiting for transfers between devices: 58.7 us -> 23 us
  Pallas kernels: 0 us -> 27.5 us
  local copies, waits for them, and re-layouts: 51.1 us -> 28.2 us
  matrix products: 33.2 us -> 13.2 us
  between operations: 14.3 us -> 0.92 us
  starting transfers between devices: 9.51 us -> 5.91 us
    psum x1 -> x0, waiting for transfers between devices: 31 us -> none  [body(): lax.psum(scale_heads(numerator, factor).astype(jnp.bfloat16), 'dp')]
    pallas_call x0 -> x1, Pallas kernels: none -> 27.5 us  [attention_call(): pl.pallas_call(attention_kernel, out_shape=(jax.ShapeDtypeStruct((NDP, ND...]
    all_gather x3 -> x0, blocking collectives: 23.6 us -> none  [the longest x1 8.64 us: body(): lax.all_gather(held_tokens, 'dp', axis=0, tiled=True)]
    dot_general x4 -> x0, matrix products: 19.9 us -> none  [the longest x1 8.04 us: holder_block(): jnp.einsum('bhe,ble->bhl', spread, keys_part, preferred_element_type=jnp....]
    gather x1 -> x0, local copies, waits for them, and re-layouts: 16.1 us -> none  [holder_block(): fetched = kv_pool[page_rows].reshape(blocks, token_span, 2 * width)]
    pmax x1 -> x0, blocking collectives: 12.4 us -> none  [body(): peak_score = lax.pmax(highest, 'dp')]
    psum x1 -> x0, blocking collectives: 10.5 us -> none  [body(): lax.psum((totals * factor).astype(jnp.bfloat16), 'dp').astype(jnp.float32)]
    another operation x3 -> x0, local copies, waits for them, and re-layouts: 9.71 us -> none  [holder_block(): jnp.tile(query_heads, (1, 1, KVH))]
  transfers between devices with their start and end apart: 3 -> 1, of which waited for: 3 -> 1; matrix products, arithmetic and copies ran while one was open for 1% -> 0% of each run, Pallas kernels for 0% -> 0%
where the time goes in v1:
time: 154 us
  blocking collectives  49 us (32%)
  local copies, waits for them, and re-layouts  28.2 us (18%)
  Pallas kernels  27.5 us (18%)
  waiting for transfers between devices  23 us (15%)
  matrix products  13.2 us (9%)
  starting transfers between devices  5.91 us (4%)
  other arithmetic  5.78 us (4%)
    all_to_all x1, blocking collectives, body(): lax.all_to_all(copies, ('dp', 'expert'), split_axis=0, concat_axis=0, til...  33.2 us
    pallas_call x1, Pallas kernels, attention_call(): pl.pallas_call(attention_kernel, out_shape=(jax.ShapeDtypeStruct((NDP, ND...  27.5 us
    all_to_all x1, waiting for transfers between devices, body(): lax.all_to_all(partial_value.astype(jnp.bfloat16), ('dp', 'expert'), spli...  23 us
    all_to_all x2, local copies, waits for them, and re-layouts, body(): lax.all_to_all(copies, ('dp', 'expert'), split_axis=0, concat_axis=0, til...  8.73 us
    all_gather x1, blocking collectives, body(): lax.all_gather(qkv_input, 'dp', axis=0, tiled=True)  8.41 us
    all_to_all x1, blocking collectives, body(): lax.all_to_all(group_qkv, 'dp', split_axis=0, concat_axis=1, tiled=True)  7.34 us
    all_to_all x1, starting transfers between devices, body(): lax.all_to_all(partial_value.astype(jnp.bfloat16), ('dp', 'expert'), spli...  5.91 us
    dot_general x1, matrix products, expert_apply(): return jnp.dot(activated, down_w, preferred_element_type=jnp.float32)  5.08 us
  transfers between devices with their start and end apart: 1, of which 1 were waited for; matrix products, arithmetic and copies ran while one was open for 0% of the time, Pallas kernels for 0%

profile of v1, /device:TPU:1, one launch (start us, length us, event | category | flops | bytes accessed | tf_op | source)
XLA Modules:
  0.0 153.5 jit_solution(15506114522187407040)
XLA Ops:
  0.7 0.9 fusion.41
  1.6 0.7 reduce_sum.64
  2.3 0.7 broadcast_divide_fusion
  3.0 0.8 select_reduce_fusion.1
  3.7 0.8 mul.75
  4.5 0.7 copy.32
  5.2 0.8 copy.33
  6.1 0.7 reshape.102
  7.3 0.1 and.27
  7.5 0.9 reshape.103
  8.4 0.9 copy.43
  9.8 27.5 %attention.1 = (bf16[4,32,720]{2,1,0:T(8,128)(2,1)S(1)}, f32[4,8,256]{2,1,0:T(8,128)S(1)}) custom-call(bf16[8,32,128]{2,1,0:T(8,128)(2,1)S(1)} %bitcast.54, s32[4,8,128]{2,1,0:T(8,128)S(1)} %pad.4.tab_ref, f32[64,128]{1,0:T(8,128)S(1)} %broadcast_in_dim.68.sink_ref, bf16[4,8,720]{2,1,0:T(8,128)(2,1)S(1)} %bitcast.55, f32[8,256]{1,0:T(8,128)S(1)} %and_select_fusion.com_ref, ...), custom_call_target="tpu_custom_call" | custom-call | tf_op jit(solution)/shard_map/attention/pallas_call | solution.py:291
  37.3 0.1 fusion.34
  37.7 0.1 copy.37
  38.0 0.2 convolution_convert_fusion.1
  38.2 1.2 broadcast_in_dim.76
  39.5 4.3 %all_to_all.28 = bf16[128,2,2880]{2,1,0:T(2,128)(2,1)} reshape(bf16[4,64,2880]{2,1,0:T(8,128)(2,1)} %broadcast_in_dim.76) | data formatting | bytes 2949120 | tf_op jit(solution)/shard_map/all_to_all | solution.py:396
  43.8 33.2 %all_to_all.40 = bf16[128,2,2880]{2,1,0:T(2,128)(2,1)} all-to-all(bf16[128,2,2880]{2,1,0:T(2,128)(2,1)} %all_to_all.28), channel_id=1, replica_groups=mesh['dp'=4,'expert'=32] {'dp','expert'}, dimensions={0} | all-to-all | bytes 2949120 | tf_op jit(solution)/shard_map/all_to_all | solution.py:396
  77.0 4.4 %all_to_all.30 = bf16[256,2880]{1,0:T(8,128)(2,1)} reshape(bf16[128,2,2880]{2,1,0:T(2,128)(2,1)} %all_to_all.40) | data formatting | bytes 2949120 | tf_op jit(solution)/shard_map/all_to_all | solution.py:396
  81.4 3.0 %fusion.7 = f32[256,384]{1,0:T(8,128)S(1)} fusion(bf16[256,2880]{1,0:T(8,128)(2,1)} %all_to_all.30, bf16[1,2880,384]{2,1,0:T(8,128)(2,1)} %param.24), kind=kOutput, calls=%fused_computation.11 | convolution fusion | flops 566329344 | bytes 4079616 | tf_op jit(solution)/shard_map/dot_general | solution.py:331
  84.4 5.1 %convolution_convert_fusion = bf16[256,2880]{0,1:T(8,128)(2,1)} fusion(bf16[1,384,2880]{1,2,0:T(8,128)(2,1)S(1)} %copy-done, bf16[256,2880]{1,0:T(8,128)(2,1)} %all_to_all.30, bf16[1,2880,384]{2,1,0:T(8,128)(2,1)} %param.25, f32[256,384]{1,0:T(8,128)S(1)} %fusion.7), kind=kOutput, calls=%fused_computation | convolution fusion | flops 1134084096 | bytes 7766016 | tf_op jit(solution)/shard_map/dot_general | solution.py:336
  89.5 2.6 %copy.39 = bf16[256,2880]{1,0:T(8,128)(2,1)} copy(bf16[256,2880]{0,1:T(8,128)(2,1)} %convolution_convert_fusion) | data formatting | bytes 2949120 | tf_op jit(solution)/shard_map/convert_element_type | solution.py:399
  92.1 4.3 %all_to_all.31 = bf16[128,2,2880]{2,1,0:T(2,128)(2,1)} reshape(bf16[256,2880]{1,0:T(8,128)(2,1)} %copy.39) | data formatting | bytes 2949120 | tf_op jit(solution)/shard_map/all_to_all | solution.py:398
  96.4 5.9 %all-to-all-start.1 = ((bf16[128,2,2880]{2,1,0:T(2,128)(2,1)}), bf16[128,2,2880]{2,1,0:T(2,128)(2,1)}, u32[]{:S(2)}, u32[]{:S(2)}) async-start(bf16[128,2,2880]{2,1,0:T(2,128)(2,1)} %all_to_all.31), calls=%async_computation.1 | async-start | bytes 3014656 | tf_op jit(solution)/shard_map/all_to_all | solution.py:398
  102.5 23.0 %all-to-all-done.1 = bf16[128,2,2880]{2,1,0:T(2,128)(2,1)} async-done(((bf16[128,2,2880]{2,1,0:T(2,128)(2,1)}), bf16[128,2,2880]{2,1,0:T(2,128)(2,1)}, u32[]{:S(2)}, u32[]{:S(2)}) %all-to-all-start.1) | async-done | bytes 1474592 | tf_op jit(solution)/shard_map/all_to_all | solution.py:398
  125.5 4.5 %reshape.107 = f32[4,64,2880]{2,1,0:T(8,128)} reshape(bf16[128,2,2880]{2,1,0:T(2,128)(2,1)} %all-to-all-done.1) | data formatting | bytes 4423680 | tf_op jit(solution)/shard_map/convert_element_type | solution.py:404
  130.0 2.1 %reduce_sum.68 = f32[64,2880]{1,0:T(8,128)S(1)} reduce(f32[4,64,2880]{2,1,0:T(8,128)} %reshape.107, f32[]{:T(128)} %constant.13.clone.1), dimensions={0}, to_apply=%region_6.7 | reduce | flops 552960 | bytes 3686404 | tf_op jit(solution)/shard_map/reduce_sum | solution.py:405
  132.1 0.6 fusion.37
  132.8 8.4 %all_gather.3 = bf16[32,2880]{1,0:T(8,128)(2,1)S(1)} all-gather(bf16[8,2880]{1,0:T(8,128)(2,1)S(1)} %fusion.39), channel_id=1, replica_groups=mesh['dp'=4,'expert'=32] {'dp'}, dimensions={0}, use_global_device_ids=true | all-gather | bytes 230400 | tf_op jit(solution)/shard_map/all_gather | solution.py:412
  141.3 4.3 %fusion.1 = bf16[4,8,1280]{2,1,0:T(8,128)(2,1)S(1)} fusion(bf16[32,2880]{1,0:T(8,128)(2,1)S(1)} %all_gather.3, bf16[2880,1280]{1,0:T(8,128)(2,1)} %param.29), kind=kOutput, calls=%fused_computation.5 | convolution fusion | flops 235970560 | bytes 7639040 | tf_op jit(solution)/shard_map/dot_general | solution.py:411
  145.5 7.3 %all_to_all.41 = bf16[4,8,1280]{2,1,0:T(8,128)(2,1)S(1)} all-to-all(bf16[4,8,1280]{2,1,0:T(8,128)(2,1)S(1)} %fusion.1), channel_id=1, replica_groups=mesh['dp'=4,'expert'=32] {'dp'}, dimensions={0} | all-to-all | bytes 163840 | tf_op jit(solution)/shard_map/all_to_all | solution.py:416
  152.9 0.6 copy.47
  (36 shorter events, 1.7 us)
Async XLA Ops:
  0.6 83.8 %copy-start = (bf16[1,384,2880]{1,2,0:T(8,128)(2,1)S(1)}, bf16[1,384,2880]{1,2,0:T(8,128)(2,1)}, u32[]{:S(2)}) copy-start(bf16[1,384,2880]{1,2,0:T(8,128)(2,1)} %param.26) | copy-start | bytes 6635524
  96.4 29.1 %all-to-all-start.1 = ((bf16[128,2,2880]{2,1,0:T(2,128)(2,1)}), bf16[128,2,2880]{2,1,0:T(2,128)(2,1)}, u32[]{:S(2)}, u32[]{:S(2)}) async-start(bf16[128,2,2880]{2,1,0:T(2,128)(2,1)} %all_to_all.31), calls=%async_computation.1 | async-start | bytes 3014656 | tf_op jit(solution)/shard_map/all_to_all | solution.py:398
  130.0 2.7 %copy-start.2 = (f32[2880]{0:T(1024)S(1)}, f32[2880]{0:T(1024)}, u32[]{:S(2)}) copy-start(f32[2880]{0:T(1024)} %param.28) | copy-start | bytes 34564
  132.7 12.8 %copy-start.1 = (bf16[8,2880]{1,0:T(8,128)(2,1)}, bf16[8,2880]{1,0:T(8,128)(2,1)S(1)}, u32[]{:S(2)}) copy-start(bf16[8,2880]{1,0:T(8,128)(2,1)S(1)} %get-tuple-element.10) | copy-start | bytes 138244

commit v2 on v1

--- a/solution.py
+++ b/solution.py
@@ -27,12 +27,6 @@
 
 S_TAB, S_Q, S_RES, S_COM, S_PAIR_N, S_PAIR_ML, S_X_N, S_X_ML, S_LHS, S_PROJ = 0, 3, 6, 9, 12, 14, 16, 18, 19, 20
 N_SEM_A = 23
-
-
-def rms_scale(values, gain):
-    wide = values.astype(jnp.float32)
-    scale = lax.rsqrt(jnp.mean(wide * wide, axis=-1, keepdims=True) + EPSILON)
-    return (wide * scale * gain).astype(jnp.bfloat16)
 
 
 def position():
@@ -327,13 +321,260 @@
     )(q_pairs, table, sink_tile, residual_blocks, combine, kv_pool, o_weight.T)
 
 
-def expert_apply(rows, gate_w, up_w, down_w):
-    gate_proj = jnp.minimum(jnp.dot(rows, gate_w, preferred_element_type=jnp.float32), LIMIT)
-    up_proj = jnp.clip(jnp.dot(rows, up_w, preferred_element_type=jnp.float32), -LIMIT, LIMIT)
-    activated = (gate_proj * jax.nn.sigmoid(1.702 * gate_proj) * (up_proj + 1.0)).astype(
-        jnp.bfloat16
+T_PAIR, T_PART, T_NEXT, T_QKV = 0, 2, 3, 4
+N_SEM_B = 7
+
+
+def normalized(blocks, gains):
+    total = sum(jnp.sum(block * block, axis=1, keepdims=True) for block in blocks)
+    width = sum(block.shape[1] for block in blocks)
+    scale = lax.rsqrt(total / width + EPSILON)
+    return [(block * scale * gain).astype(BF16) for block, gain in zip(blocks, gains)]
+
+
+def expert_kernel(
+    stream_ref, com_ref, mgain_ref, again_ref, wg_hbm, wu_hbm, wd_hbm, wq_hbm,
+    next_out, qkv_out,
+    wg, wu, wd, wq, xin, outbox, arr, gate, up, osend, orecv, rbuf, ret, part_s, part_r, nextb, nextf, qbuf,
+    load_sem, send_sem, recv_sem, d_send, d_recv, f_send, f_recv, r_send, r_recv,
+):
+    dp, z, c, expert = position()
+    sems = (send_sem, recv_sem)
+    count = arr.shape[2]
+    slots = arr.shape[3]
+    width = arr.shape[4]
+    block = c * 2 + z
+    loads = [
+        pltpu.make_async_copy(src, dst, load_sem.at[i])
+        for i, (src, dst) in enumerate(((wg_hbm, wg), (wu_hbm, wu), (wd_hbm, wd), (wq_hbm, wq)))
+    ]
+    for load in loads:
+        load.start()
+
+    barrier = pltpu.get_barrier_semaphore()
+    for offset in (1, 2, 3):
+        pl.semaphore_signal(barrier, inc=1, device_id=(group_peer(z, c, offset), expert), device_id_type=MESH)
+
+    def greet(i, carry):
+        pl.semaphore_signal(barrier, inc=1, device_id=(dp, lax.rem(expert + i, count)), device_id_type=MESH)
+        return carry
+
+    lax.fori_loop(1, count, greet, 0)
+
+    rows = [stream_ref[k].astype(F32) for k in range(NDP)]
+    for k, value in enumerate(normalized(rows, [mgain_ref[k] for k in range(NDP)])):
+        xin[k] = value
+    share = jnp.concatenate([com_ref[d] for d in range(NDP)], axis=0)
+    picks = (share > 0).astype(F32).T.astype(BF16)
+    for j in range(2):
+        picked = jnp.dot(picks, xin[2 * c + j], preferred_element_type=F32).astype(BF16)
+        outbox[j] = picked.reshape(count, slots, width)
+    pl.semaphore_wait(barrier, count + 2)
+
+    sent = []
+
+    def send(src, dst, number, landed, offset):
+        copy = remote(src, dst, sems, number, landed, (group_peer(z, c, offset), expert))
+        copy.start()
+        sent.append(copy)
+        return copy
+
+    def dispatch(to, slot):
+        return remote(outbox.at[:, to], arr.at[c, :, slot], (d_send, d_recv), to, slot, (dp, to))
+
+    def forward(source):
+        return remote(
+            arr.at[c, :, source], arr.at[c, :, source], (f_send, f_recv), source, source,
+            (group_peer(z, c, 1), expert),
+        )
+
+    def giveback(j, to, slot):
+        return remote(rbuf.at[j, to], ret.at[j, slot], (r_send.at[j], r_recv.at[j]), to, slot, (dp, to))
+
+    def start_dispatch(i, carry):
+        dispatch(lax.rem(expert + i, count), expert).start()
+        return carry
+
+    lax.fori_loop(1, count, start_dispatch, 0)
+    for j in range(2):
+        arr[c, j, expert] = outbox[j, expert]
+    forward(expert).start()
+
+    def pass_on(i, carry):
+        source = lax.rem(expert + count - i, count)
+        dispatch(source, source).wait_recv()
+        forward(source).start()
+        return carry
+
+    lax.fori_loop(1, count, pass_on, 0)
+    loads[0].wait()
+    loads[1].wait()
+
+    def project(half, first):
+        for j in range(2):
+            rows = arr[half, j].reshape(count * slots, width)
+            for total, weight in ((gate, wg), (up, wu)):
+                value = jnp.dot(rows, weight[2 * half + j], preferred_element_type=F32)
+                if first and j == 0:
+                    total[...] = value
+                else:
+                    total[...] += value
+
+    project(c, True)
+
+    def arrived(source, carry):
+        forward(source).wait_recv()
+        return carry
+
+    lax.fori_loop(0, count, arrived, 0)
+    project(1 - c, False)
+    gated = jnp.minimum(gate[...], LIMIT)
+    lifted = jnp.clip(up[...], -LIMIT, LIMIT)
+    activated = (gated * jax.nn.sigmoid(1.702 * gated) * (lifted + 1.0)).astype(BF16)
+    loads[2].wait()
+
+    def down(k):
+        return lax.dot_general(activated, wd[k], (((1,), (1,)), ((), ())), preferred_element_type=F32)
+
+    pair_in = []
+    for j in range(2):
+        osend[j] = down(2 * (1 - c) + j).astype(BF16)
+        pair_in.append(send(osend.at[j], orecv.at[j], T_PAIR + j, T_PAIR + j, 1))
+    for j in range(2):
+        own = down(2 * c + j)
+        pair_in[j].wait_recv()
+        rbuf[j] = (own + orecv[j].astype(F32)).astype(BF16).reshape(count, slots, width)
+
+        def start_return(i, carry):
+            giveback(j, lax.rem(expert + i, count), expert).start()
+            return carry
+
+        lax.fori_loop(1, count, start_return, 0)
+        ret[j, expert] = rbuf[j, expert]
+
+    high = share.astype(BF16)
+    low = (share - high.astype(F32)).astype(BF16)
+    both = jnp.concatenate([high, low], axis=0)
+    group_rows = share.shape[0]
+    for j in range(2):
+
+        def returned(source, carry):
+            @pl.when(source != expert)
+            def _():
+                giveback(j, source, source).wait_recv()
+
+            return carry
+
+        lax.fori_loop(0, count, returned, 0)
+        mixed = jnp.dot(both, ret[j].reshape(count * slots, width), preferred_element_type=F32)
+        part_s[j] = (mixed[:group_rows] + mixed[group_rows:]).astype(BF16)
+    send(part_s, part_r, T_PART, T_PART, 2).wait_recv()
+    for j in range(2):
+        moe_out = part_s[j].astype(F32) + part_r[j].astype(F32)
+        nextb[c, j] = (stream_ref[2 * c + j].astype(F32) + moe_out).astype(BF16)
+    next_in = send(nextb.at[c], nextb.at[c], T_NEXT, T_NEXT, 1)
+    next_in.wait_recv()
+    rows = [nextb[k // 2, k % 2].astype(F32) for k in range(NDP)]
+    for k in range(NDP):
+        nextf[k] = rows[k]
+    inputs = normalized(rows, [again_ref[k] for k in range(NDP)])
+    loads[3].wait()
+    qkv = sum(jnp.dot(inputs[k], wq[k], preferred_element_type=F32) for k in range(NDP))
+    columns = qkv.shape[1]
+    for d in range(NDP):
+        qbuf[d] = qkv[ROWS * d : ROWS * d + ROWS].astype(BF16)
+    own_columns = pl.ds(pl.multiple_of(dp * columns, 128), columns)
+    qkv_in = []
+    for offset in (2, 3, 1):
+        peer = group_peer(z, c, offset)
+        theirs = lax.rem(peer, 2) * 2 + lax.div(peer, 2)
+        qkv_in.append(
+            send(qbuf.at[theirs], qkv_out.at[:, own_columns], T_QKV + offset - 1, T_QKV + offset - 1, offset)
+        )
+    qkv_out[:, own_columns] = qbuf[block]
+    start = pl.multiple_of(block * ROWS, ROWS)
+    for k in range(NDP):
+        next_out[:, width * k : width * k + width] = nextf[k, pl.ds(start, ROWS), :].astype(BF16)
+
+    def all_sent(i, carry):
+        to = lax.rem(expert + i, count)
+        dispatch(to, expert).wait_send()
+        for j in range(2):
+            giveback(j, to, expert).wait_send()
+        return carry
+
+    lax.fori_loop(1, count, all_sent, 0)
+
+    def all_passed(source, carry):
+        forward(source).wait_send()
+        return carry
+
+    lax.fori_loop(0, count, all_passed, 0)
+    for copy in sent:
+        copy.wait_send()
+    for copy in qkv_in:
+        copy.wait_recv()
+
+
+def expert_call(streams, tables, moe_gain, attn_gain, w_gate, w_up, w_down, qkv_weight, count):
+    width = streams.shape[2]
+    hidden = w_gate.shape[2]
+    columns = qkv_weight.shape[1]
+    slots = tables.shape[2] // count
+    vmem = pl.BlockSpec(memory_space=pltpu.VMEM)
+    hbm = pl.BlockSpec(memory_space=pl.ANY)
+    group_rows = NDP * ROWS
+    all_slots = count * slots
+    dma = pltpu.SemaphoreType.DMA
+    return pl.pallas_call(
+        expert_kernel,
+        out_shape=(
+            jax.ShapeDtypeStruct((ROWS, NDP * width), BF16),
+            jax.ShapeDtypeStruct((ROWS, NDP * columns), BF16),
+        ),
+        in_specs=[vmem] * 4 + [hbm] * 4,
+        out_specs=(vmem, vmem),
+        scratch_shapes=[
+            pltpu.VMEM((NDP, width, hidden), BF16),
+            pltpu.VMEM((NDP, width, hidden), BF16),
+            pltpu.VMEM((NDP, width, hidden), BF16),
+            pltpu.VMEM((NDP, width, columns), BF16),
+            pltpu.VMEM((NDP, group_rows, width), BF16),
+            pltpu.VMEM((2, count, slots, width), BF16),
+            pltpu.VMEM((2, 2, count, slots, width), BF16),
+            pltpu.VMEM((all_slots, hidden), F32),
+            pltpu.VMEM((all_slots, hidden), F32),
+            pltpu.VMEM((2, all_slots, width), BF16),
+            pltpu.VMEM((2, all_slots, width), BF16),
+            pltpu.VMEM((2, count, slots, width), BF16),
+            pltpu.VMEM((2, count, slots, width), BF16),
+            pltpu.VMEM((2, group_rows, width), BF16),
+            pltpu.VMEM((2, group_rows, width), BF16),
+            pltpu.VMEM((2, 2, group_rows, width), BF16),
+            pltpu.VMEM((NDP, group_rows, width), F32),
+            pltpu.VMEM((NDP, ROWS, columns), BF16),
+            dma((4,)),
+            dma((N_SEM_B,)),
+            dma((N_SEM_B,)),
+            dma((count,)),
+            dma((count,)),
+            dma((count,)),
+            dma((count,)),
+            dma((2, count)),
+            dma((2, count)),
+        ],
+        compiler_params=pltpu.CompilerParams(collective_id=1, has_side_effects=True, vmem_limit_bytes=56 * 2**20),
+        name="experts",
+    )(
+        streams,
+        tables,
+        moe_gain.reshape(NDP, 1, width),
+        attn_gain.reshape(NDP, 1, width),
+        w_gate.reshape(NDP, width, hidden),
+        w_up.reshape(NDP, width, hidden),
+        w_down[0].T.reshape(NDP, width, hidden),
+        qkv_weight.reshape(NDP, width, columns),
     )
-    return jnp.dot(activated, down_w, preferred_element_type=jnp.float32)
 
 
 def combine_table(route_ids, route_weights, experts_count, capacity, block):
@@ -367,7 +608,6 @@
     attn_gain,
     qkv_weight,
 ):
-    dp_count = lax.axis_size("dp")
     experts_count = lax.axis_size("expert")
     own_rows = queries.shape[0]
     holder = lax.axis_index("dp")
@@ -377,44 +617,9 @@
     streams, tables = attention_call(
         queries, kv_pool, page_table, held_tokens, sinks, residual, table, o_weight
     )
-    stream = lax.dynamic_slice_in_dim(streams, block * own_rows, own_rows, 1)
-    stream = stream.transpose(1, 0, 2).reshape(own_rows, -1)
-    moe_input = rms_scale(stream, moe_gain)
-    own = lax.dynamic_index_in_dim(tables, block, 0, keepdims=False)
-    own = own.reshape(own_rows, experts_count, NDP, capacity)
-    combine = jnp.sum(own, axis=2).reshape(own_rows, experts_count * capacity)
-    dispatch = (combine > 0).astype(jnp.bfloat16)
-    send_rows = jnp.einsum(
-        "rc,rd->cd", dispatch, moe_input, preferred_element_type=jnp.float32
-    ).astype(jnp.bfloat16)
-    gate_local = w_gate[0]
-    up_local = w_up[0]
-    down_local = w_down[0]
-    copies = jnp.broadcast_to(send_rows[None], (dp_count,) + send_rows.shape).reshape(
-        dp_count * send_rows.shape[0], send_rows.shape[1]
+    return expert_call(
+        streams, tables, moe_gain, attn_gain, w_gate, w_up, w_down, qkv_weight, experts_count
     )
-    arrived = lax.all_to_all(copies, ("dp", "expert"), split_axis=0, concat_axis=0, tiled=True)
-    partial_value = expert_apply(arrived, gate_local, up_local, down_local)
-    came_back = lax.all_to_all(
-        partial_value.astype(jnp.bfloat16),
-        ("dp", "expert"),
-        split_axis=0,
-        concat_axis=0,
-        tiled=True,
-    ).astype(partial_value.dtype)
-    returned = jnp.sum(came_back.reshape(dp_count, send_rows.shape[0], send_rows.shape[1]), axis=0)
-    moe_out = jnp.dot(
-        combine, returned, precision=lax.Precision.HIGHEST, preferred_element_type=jnp.float32
-    )
-    next_stream = (stream.astype(jnp.float32) + moe_out).astype(jnp.bfloat16)
-    qkv_input = rms_scale(next_stream, attn_gain)
-    group_qkv = jnp.dot(
-        lax.all_gather(qkv_input, "dp", axis=0, tiled=True),
-        qkv_weight,
-        preferred_element_type=jnp.float32,
-    ).astype(jnp.bfloat16)
-    next_qkv = lax.all_to_all(group_qkv, "dp", split_axis=0, concat_axis=1, tiled=True)
-    return (next_stream, next_qkv)
 
 
 def solution(mesh):

time: 154 us -> 91.7 us (0.60)
  Pallas kernels: 27.5 us -> 76.7 us
  blocking collectives: 49 us -> 0 us
  waiting for transfers between devices: 23 us -> 0 us
  local copies, waits for them, and re-layouts: 28.2 us -> 10.6 us
  matrix products: 13.2 us -> 0 us
  starting transfers between devices: 5.91 us -> 0 us
  other arithmetic: 5.78 us -> 3.1 us
    pallas_call x0 -> x1, Pallas kernels: none -> 49.2 us  [expert_call(): pl.pallas_call(expert_kernel, out_shape=(jax.ShapeDtypeStruct((ROWS, NDP...]
    all_to_all x2 -> x0, blocking collectives: 40.6 us -> none  [the longest x1 33.2 us: body(): lax.all_to_all(copies, ('dp', 'expert'), split_axis=0, concat_axis=0, til...]
    all_to_all x1 -> x0, waiting for transfers between devices: 23 us -> none  [body(): lax.all_to_all(partial_value.astype(jnp.bfloat16), ('dp', 'expert'), spli...]
    dot_general x5 -> x0, matrix products: 13.2 us -> none  [the longest x1 5.08 us: expert_apply(): return jnp.dot(activated, down_w, preferred_element_type=jnp.float32)]
    all_to_all x3 -> x0, local copies, waits for them, and re-layouts: 13 us -> none  [the longest x2 8.73 us: body(): lax.all_to_all(copies, ('dp', 'expert'), split_axis=0, concat_axis=0, til...]
    all_gather x1 -> x0, blocking collectives: 8.41 us -> none  [body(): lax.all_gather(qkv_input, 'dp', axis=0, tiled=True)]
    convert_element_type x5 -> x0, local copies, waits for them, and re-layouts: 7.34 us -> none  [the longest x1 4.52 us: body(): came_back = lax.all_to_all(partial_value.astype(jnp.bfloat16), ('dp', 'ex...]
    all_to_all x1 -> x0, starting transfers between devices: 5.91 us -> none  [body(): lax.all_to_all(partial_value.astype(jnp.bfloat16), ('dp', 'expert'), spli...]
  transfers between devices with their start and end apart: 1 -> 0, of which waited for: 1 -> 0; matrix products, arithmetic and copies ran while one was open for 0% -> 0% of each run, Pallas kernels for 0% -> 0%
where the time goes in v2:
time: 91.7 us; the launch traced here: 91.2 us
  Pallas kernels  76.7 us (84%)
  local copies, waits for them, and re-layouts  10.6 us (12%)
  other arithmetic  3.1 us (3%)
    pallas_call x1, Pallas kernels, expert_call(): pl.pallas_call(expert_kernel, out_shape=(jax.ShapeDtypeStruct((ROWS, NDP...  49.2 us
    pallas_call x1, Pallas kernels, attention_call(): pl.pallas_call(attention_kernel, out_shape=(jax.ShapeDtypeStruct((NDP, ND...  27.5 us
    unnamed x12, local copies, waits for them, and re-layouts  5.8 us

profile of v2, /device:TPU:1, one launch (start us, length us, event | category | flops | bytes accessed | tf_op | source)
XLA Modules:
  0.0 91.2 jit_solution(7423036125422735315)
XLA Ops:
  0.6 0.8 fusion
  1.4 0.1 select_reduce_fusion
  1.5 0.1 eq.39
  1.6 0.1 eq.40
  1.7 0.1 and.26
  1.8 0.1 and.27
  2.0 0.7 reduce_sum.28
  2.7 0.7 broadcast_divide_fusion
  3.4 0.8 select_reduce_fusion.1
  4.1 0.1 broadcast_in_dim.63
  4.2 0.1 broadcast_in_dim.64
  4.4 0.1 eq.37
  4.5 0.9 %reshape.61 = bf16[8,4,720]{2,1,0:T(4,128)(2,1)S(1)} reshape(bf16[8,2880]{1,0:T(8,128)(2,1)} %param.20) | data formatting | bytes 92160 | tf_op jit(solution)/shard_map/reshape | solution.py:281
  5.4 0.9 copy.35
  6.2 0.7 copy.28
  7.0 0.8 copy.29
  7.7 0.1 add_bitcast_fusion
  7.8 0.7 reshape.60
  8.6 0.1 copy.30
  8.7 0.1 broadcast_in_dim.57
  8.7 0.1 broadcast_in_dim.58.sink_ref
  8.8 27.5 %attention.1 = (bf16[4,32,720]{2,1,0:T(8,128)(2,1)S(1)}, f32[4,8,256]{2,1,0:T(8,128)S(1)}) custom-call(bf16[8,32,128]{2,1,0:T(8,128)(2,1)S(1)} %bitcast.20, s32[4,8,128]{2,1,0:T(8,128)S(1)} %pad.4.tab_ref, f32[64,128]{1,0:T(8,128)S(1)} %broadcast_in_dim.58.sink_ref, bf16[4,8,720]{2,1,0:T(8,128)(2,1)S(1)} %bitcast.21, f32[8,256]{1,0:T(8,128)S(1)} %and_select_fusion.com_ref, ...), custom_call_target="tpu_custom_call" | custom-call | tf_op jit(solution)/shard_map/attention/pallas_call | solution.py:285
  36.4 0.0 copy-start
  36.4 0.7 copy-done
  37.0 0.6 copy-done.1
  37.7 0.0 copy-done.2
  37.7 0.7 reshape.62.mgain_ref
  38.3 0.0 copy-done.3
  38.4 0.7 reshape.63.again_ref
  39.0 49.2 %experts.1 = (bf16[8,2880]{1,0:T(8,128)(2,1)}, bf16[8,5120]{1,0:T(8,128)(2,1)}) custom-call(bf16[4,32,720]{2,1,0:T(8,128)(2,1)} %copy-done, f32[4,8,256]{2,1,0:T(8,128)} %copy-done.1, f32[4,1,720]{2,1,0:T(1,128)} %reshape.62.mgain_ref, f32[4,1,720]{2,1,0:T(1,128)} %reshape.63.again_ref, bf16[4,720,384]{2,1,0:T(8,128)(2,1)} %bitcast.24, ...), custom_call_target="tpu_custom_call" | custom-call | tf_op jit(solution)/shard_map/experts/pallas_call | solution.py:529
  88.2 1.4 %copy.39 = bf16[8,2880]{1,0:T(8,128)(2,1)} copy(bf16[8,2880]{1,0:T(8,128)(2,1)} %get-tuple-element.8) | data formatting | bytes 92160
  89.6 1.5 %copy.40 = bf16[8,5120]{1,0:T(8,128)(2,1)} copy(bf16[8,5120]{1,0:T(8,128)(2,1)} %get-tuple-element.9) | data formatting | bytes 163840
  (9 shorter events, 0.0 us)
Async XLA Ops:
  8.8 28.8 %copy-start.2 = (f32[2880]{0:T(1024)S(1)}, f32[2880]{0:T(1024)}, u32[]{:S(2)}) copy-start(f32[2880]{0:T(1024)} %param.23) | copy-start | bytes 34564
  8.8 29.5 %copy-start.3 = (f32[2880]{0:T(1024)S(1)}, f32[2880]{0:T(1024)}, u32[]{:S(2)}) copy-start(f32[2880]{0:T(1024)} %param.28) | copy-start | bytes 34564
  36.4 0.7 copy-start
  37.0 0.6 copy-start.1

commit v3 on v2

v3 whole, which is shorter than its diff:
```python
import math

import jax
import jax.numpy as jnp
from jax import lax
from jax.experimental import pallas as pl
from jax.experimental.pallas import tpu as pltpu
from jax.sharding import PartitionSpec as P

HEADS = 64
KVH = 8
HD = 64
TOP = 4
PAGE = 16
PPH = 16
SPAN = PPH * PAGE
WIDE = KVH * HD
PAIR = 2 * HD
ROWS = 8
NDP = 4

EPSILON = 1e-05
LIMIT = 7.0
MESH = pl.DeviceIdType.MESH
F32 = jnp.float32
BF16 = jnp.bfloat16

S_TAB, S_HELD, S_Q, S_RES, S_COM, S_PAIR_N, S_PAIR_ML, S_X_N, S_X_ML, S_LHS, S_PROJ = 0, 3, 6, 9, 12, 15, 17, 19, 21, 22, 23
S_OUT, S_PART, S_NEXT, S_QKV = 26, 28, 29, 30
N_SEM = 33
L_TAB, L_HELD, L_Q, L_POOL, L_SINK, L_IDS, L_WEIGHTS, L_RES, L_OW, L_MGAIN, L_GATE, L_UP, L_DOWN, L_AGAIN, L_QKV = range(15)


def position():
    dp = lax.axis_index("dp")
    expert = lax.axis_index("expert")
    return dp, lax.div(dp, 2), lax.rem(dp, 2), expert


def group_peer(z, c, offset):
    return lax.rem(z + offset // 2, 2) * 2 + lax.rem(c + offset % 2, 2)


def remote(src, dst, sems, sent, landed, device):
    return pltpu.make_async_remote_copy(
        src_ref=src,
        dst_ref=dst,
        send_sem=sems[0].at[sent],
        recv_sem=sems[1].at[landed],
        device_id=device,
        device_id_type=MESH,
    )


def spread_queries(wide):
    turned = pltpu.roll(wide, HD, 1)
    row = lax.broadcasted_iota(jnp.int32, (HEADS // 2, PAIR), 0)
    lane = lax.broadcasted_iota(jnp.int32, (HEADS // 2, PAIR), 1)
    odd_group = lax.rem(lax.div(row, 4), 2) == 1
    own_half = (lane >= HD) == odd_group
    even = jnp.where(own_half, jnp.where(odd_group, turned, wide), 0.0)
    odd = jnp.where(own_half, jnp.where(odd_group, wide, turned), 0.0)
    tile = lax.div(row, 8)
    parts = []
    for heads in (even, odd):
        parts.append(jnp.concatenate([jnp.where(tile == t, heads, 0.0) for t in range(4)], axis=1))
    return jnp.concatenate(parts, axis=0).astype(BF16)


def fold_values(wide):
    row = lax.broadcasted_iota(jnp.int32, (HEADS // 2, PAIR), 0)
    lane = lax.broadcasted_iota(jnp.int32, (HEADS // 2, PAIR), 1)
    odd_group = lax.rem(lax.div(row, 4), 2) == 1

    def own_tiles(base):
        return jnp.concatenate(
            [wide[base + 8 * t : base + 8 * t + 8, PAIR * t : PAIR * t + PAIR] for t in range(4)], axis=0
        )

    even, odd = own_tiles(0), own_tiles(HEADS // 2)
    even = jnp.where(odd_group, pltpu.roll(even, HD, 1), even)
    odd = jnp.where(odd_group, odd, pltpu.roll(odd, HD, 1))
    return jnp.where(lane < HD, even, odd)


def pair_columns(column):
    lane = lax.broadcasted_iota(jnp.int32, (HEADS // 2, PAIR), 1)
    return jnp.where(lane < HD, column[: HEADS // 2], column[HEADS // 2 :])


def normalized(blocks, gains):
    total = sum(jnp.sum(block * block, axis=1, keepdims=True) for block in blocks)
    width = sum(block.shape[1] for block in blocks)
    scale = lax.rsqrt(total / width + EPSILON)
    return [(block * scale * gain).astype(BF16) for block, gain in zip(blocks, gains)]


def attend(queries, tables, counts, holder, pool, rows, write):
    token = lax.broadcasted_iota(jnp.int32, (HEADS, SPAN), 1)
    scores, held = [], []
    for row in rows:
        keys = jnp.concatenate([pool[tables[row, holder, page], :, :WIDE] for page in range(PPH)], axis=0)
        start = pl.multiple_of(row * (HEADS // 2), HEADS // 2)
        spread = spread_queries(queries[pl.ds(start, HEADS // 2), :])
        scores.append(
            lax.dot_general(spread, keys, (((1,), (1,)), ((), ())), preferred_element_type=F32)
            * (1.0 / math.sqrt(HD))
        )
        held.append(token < counts[holder, row])
    weights, highs, sums = [], [], []
    for score, usable in zip(scores, held):
        high = jnp.max(jnp.where(usable, score, -1e30), axis=1, keepdims=True)
        weight = jnp.where(usable, jnp.exp(score - high), 0.0)
        highs.append(high)
        sums.append(jnp.sum(weight, axis=1, keepdims=True))
        weights.append(weight.astype(BF16))
    results = []
    for row, weight in zip(rows, weights):
        values = jnp.concatenate([pool[tables[row, holder, page], :, WIDE:] for page in range(PPH)], axis=0)
        results.append(fold_values(jnp.dot(weight, values, preferred_element_type=F32)))
    for row, result, high, total in zip(rows, results, highs, sums):
        write(row, result, high, total)


def sink_columns(sinks):
    row = lax.broadcasted_iota(jnp.int32, (HEADS, HEADS), 0)
    lane = lax.broadcasted_iota(jnp.int32, (HEADS, HEADS), 1)
    half = HEADS // 2
    head = jnp.where(row < half, 2 * row, 2 * (row - half) + 1)
    return jnp.sum(jnp.where(lane == head, sinks, 0.0), axis=1, keepdims=True)


def combine_rows(ids, weights, table, block, slots):
    capacity = slots // NDP
    lane = lax.broadcasted_iota(jnp.int32, (1, table.shape[1]), 1)
    of_expert, at_slot = lax.div(lane, slots), lax.rem(lane, slots)
    taken = jnp.zeros_like(lane)
    for row in range(ROWS):
        hit = jnp.zeros_like(lane)
        weight = jnp.zeros(lane.shape, F32)
        total = jnp.zeros(lane.shape, F32)
        for k in range(TOP):
            match = of_expert == ids[k, row]
            hit = jnp.where(match, 1, hit)
            weight = jnp.where(match, weights[k, row], weight)
            total = total + weights[k, row]
        at = (hit == 1) & (at_slot == block * capacity + taken)
        table[row : row + 1, :] = jnp.where(at, weight / total, 0.0)
        taken = taken + hit


STEP = 4


def layer_kernel(
    q_hbm, pool_hbm, tab_hbm, held_hbm, sink_hbm, res_hbm, ids_hbm, weights_hbm, mgain_hbm,
    wg_hbm, wu_hbm, wd_hbm, ow_hbm, again_hbm, wq_hbm,
    next_out, qkv_out,
    pool, ow, wg, wu, wd, wq,
    tabs, helds, ids, weights, sinks, mgain, again, qraw, qwide, resraw, comown, comall,
    keep_n, keep_ml, send_n, send_ml, recv_n, recv_ml, xs_n, xs_ml, xr_n, xr_ml, att, lhs, pall, stream,
    xin, outbox, arr, gate, up, osend, orecv, rbuf, ret, part_s, part_r, nextb, nextf, qbuf,
    load_sem, send_sem, recv_sem, d_send, d_recv, f_send, f_recv, r_send, r_recv,
):
    dp, z, c, expert = position()
    sems = (send_sem, recv_sem)
    count, slots, width = arr.shape[2], arr.shape[3], arr.shape[4]
    block = c * 2 + z

    barrier = pltpu.get_barrier_semaphore()
    for offset in (1, 2, 3):
        pl.semaphore_signal(barrier, inc=1, device_id=(group_peer(z, c, offset), expert), device_id_type=MESH)

    def greet(i, carry):
        pl.semaphore_signal(barrier, inc=1, device_id=(dp, lax.rem(expert + i, count)), device_id_type=MESH)
        return carry

    lax.fori_loop(1, count, greet, 0)
    loads = {}
    for number, src, dst in (
        (L_TAB, tab_hbm, tabs.at[dp]),
        (L_HELD, held_hbm, helds.at[dp]),
        (L_Q, q_hbm, qraw.at[dp]),
        (L_POOL, pool_hbm, pool),
        (L_SINK, sink_hbm, sinks),
        (L_IDS, ids_hbm, ids),
        (L_WEIGHTS, weights_hbm, weights),
        (L_RES, res_hbm, resraw.at[block]),
        (L_OW, ow_hbm, ow),
        (L_MGAIN, mgain_hbm, mgain),
        (L_GATE, wg_hbm, wg),
        (L_UP, wu_hbm, wu),
        (L_DOWN, wd_hbm, wd),
        (L_AGAIN, again_hbm, again),
        (L_QKV, wq_hbm, wq),
    ):
        loads[number] = pltpu.make_async_copy(src, dst, load_sem.at[number])
        loads[number].start()

    sent = []

    def send(src, dst, number, landed, offset):
        copy = remote(src, dst, sems, number, landed, (group_peer(z, c, offset), expert))
        copy.start()
        sent.append(copy)
        return copy

    lane = lax.broadcasted_iota(jnp.int32, (HEADS, PAIR), 1)

    def run_block(offset, number, numerators, stats):
        at = group_peer(z, c, offset)
        half = z if number == 0 else 1 - z
        stats[number] = jnp.zeros((HEADS, PAIR), F32)
        for pair in range(HEADS // 2):
            qwide[pl.ds(pair, ROWS, stride=HEADS // 2), :] = qraw[at, :, PAIR * pair : PAIR * pair + PAIR].astype(F32)

        def write(row, result, high, total):
            numerators[number, row] = result.astype(numerators.dtype)
            place = half * ROWS + row
            tile = jnp.where(lane == place, high, stats[number])
            stats[number] = jnp.where(lane == place + HD, total, tile)

        def step(index, carry):
            rows = [index * STEP + i for i in range(STEP)]
            attend(qwide, tabs.at[at], helds.at[at], dp, pool, rows, write)
            return carry

        lax.fori_loop(0, ROWS // STEP, step, 0)

    tab_in, held_in, q_in, res_in, com_in = {}, {}, {}, {}, {}

    def fetch_block(offset):
        tab_in[offset].wait_recv()
        held_in[offset].wait_recv()
        q_in[offset].wait_recv()

    def send_pair(number):
        return (
            send(send_n.at[number], recv_n.at[number], S_PAIR_N + number, S_PAIR_N + number, 1),
            send(send_ml.at[number], recv_ml.at[number], S_PAIR_ML + number, S_PAIR_ML + number, 1),
        )

    def factors(tile, number):
        half = z if number == 0 else 1 - z
        return pltpu.roll(tile, lax.rem(PAIR - half * ROWS, PAIR), 1)

    def merge_pair(number, incoming):
        for copy in incoming:
            copy.wait_recv()
        mine, other = keep_ml[number], recv_ml[number]
        high = jnp.maximum(mine, other)
        left, right = jnp.exp(mine - high), jnp.exp(other - high)
        total = mine * pltpu.roll(left, HD, 1) + other * pltpu.roll(right, HD, 1)
        keep_ml[number] = jnp.where(lane < HD, high, total)
        left, right = factors(left, number), factors(right, number)
        for row in range(ROWS):
            merged = keep_n[number, row] * pair_columns(left[:, row : row + 1]) + recv_n[number, row].astype(
                F32
            ) * pair_columns(right[:, row : row + 1])
            keep_n[number, row] = merged
            xs_n[number, row] = merged.astype(BF16)
        return send(xs_n.at[number], xr_n.at[1 - number], S_X_N + number, S_X_N + 1 - number, 2)

    pl.semaphore_wait(barrier, count + 2)
    for offset in (2, 3, 1):
        tab_in[offset] = send(tab_hbm, tabs.at[dp], S_TAB + offset - 1, S_TAB + offset - 1, offset)
        held_in[offset] = send(held_hbm, helds.at[dp], S_HELD + offset - 1, S_HELD + offset - 1, offset)
        q_in[offset] = send(q_hbm, qraw.at[dp], S_Q + offset - 1, S_Q + offset - 1, offset)
    for offset in (2, 3, 1):
        res_in[offset] = send(res_hbm, resraw.at[block], S_RES + offset - 1, S_RES + offset - 1, offset)
    for number in (L_IDS, L_WEIGHTS):
        loads[number].wait()
    combine_rows(ids, weights, comown, block, slots)
    comall[block] = comown[...]
    for offset in (2, 3, 1):
        com_in[offset] = send(comown, comall.at[block], S_COM + offset - 1, S_COM + offset - 1, offset)

    for number in (L_TAB, L_HELD, L_Q, L_POOL):
        loads[number].wait()
    run_block(0, 0, keep_n, keep_ml)
    fetch_block(1)
    run_block(1, 0, send_n, send_ml)
    pair_in = [send_pair(0)]
    fetch_block(3)
    run_block(3, 1, send_n, send_ml)
    pair_in.append(send_pair(1))
    cross_in = [merge_pair(0, pair_in[0])]
    fetch_block(2)
    run_block(2, 1, keep_n, keep_ml)
    cross_in.append(merge_pair(1, pair_in[1]))
    xs_ml[...] = keep_ml[0] + keep_ml[1]
    cross_ml = send(xs_ml, xr_ml, S_X_ML, S_X_ML, 2)

    cross_ml.wait_recv()
    loads[L_SINK].wait()
    mine, other, sink = xs_ml[...], xr_ml[...], sink_columns(sinks[...])
    top = jnp.maximum(jnp.maximum(mine, other), sink)
    left, right = jnp.exp(mine - top), jnp.exp(other - top)
    total = mine * pltpu.roll(left, HD, 1) + other * pltpu.roll(right, HD, 1)
    below = pltpu.roll(total, HD, 1) + jnp.exp(sink - top)
    left, right = left / below, right / below
    for number in (0, 1):
        cross_in[1 - number].wait_recv()
        one, two = factors(left, number), factors(right, number)
        half = z if number == 0 else 1 - z
        for row in range(ROWS):
            attention = keep_n[number, row] * pair_columns(one[:, row : row + 1]) + xr_n[number, row].astype(
                F32
            ) * pair_columns(two[:, row : row + 1])
            start = pl.multiple_of((half * ROWS + row) * (HEADS // 2), HEADS // 2)
            att[pl.ds(start, HEADS // 2), :] = attention
    for pair in range(HEADS // 2):
        lhs[c, :, PAIR * pair : PAIR * pair + PAIR] = att[pl.ds(pair, 2 * ROWS, stride=HEADS // 2), :].astype(BF16)
    lhs_in = send(lhs.at[c], lhs.at[c], S_LHS, S_LHS, 1)
    loads[L_OW].wait()
    lhs_in.wait_recv()
    rows = jnp.concatenate([lhs[0], lhs[1]], axis=0)
    projected = lax.dot_general(rows, ow[...], (((1,), (1,)), ((), ())), preferred_element_type=F32)
    pall[dp] = projected.astype(BF16)
    proj_in = [
        send(pall.at[dp], pall.at[dp], S_PROJ + offset - 1, S_PROJ + offset - 1, offset) for offset in (2, 3, 1)
    ]
    for offset in (1, 2, 3):
        res_in[offset].wait_recv()
        com_in[offset].wait_recv()
    for copy in proj_in:
        copy.wait_recv()
    loads[L_RES].wait()
    loads[L_MGAIN].wait()
    rows = []
    for k in range(NDP):
        residual = jnp.concatenate(
            [resraw[d, :, width * k : width * k + width].astype(F32) for d in range(NDP)], axis=0
        )
        rows.append((residual + pall[k].astype(F32)).astype(BF16).astype(F32))
        stream[k] = rows[k]
    gains = [mgain[:, width * k : width * k + width] for k in range(NDP)]
    for k, value in enumerate(normalized(rows, gains)):
        xin[k] = value
    share = jnp.concatenate([comall[d] for d in range(NDP)], axis=0)
    picks = (share > 0).astype(F32).T.astype(BF16)
    for j in range(2):
        picked = jnp.dot(picks, xin[2 * c + j], preferred_element_type=F32).astype(BF16)
        outbox[j] = picked.reshape(count, slots, width)

    def dispatch(to, slot):
        return remote(outbox.at[:, to], arr.at[c, :, slot], (d_send, d_recv), to, slot, (dp, to))

    def forward(source):
        return remote(
            arr.at[c, :, source], arr.at[c, :, source], (f_send, f_recv), source, source,
            (group_peer(z, c, 1), expert),
        )

    def giveback(j, to, slot):
        return remote(rbuf.at[j, to], ret.at[j, slot], (r_send.at[j], r_recv.at[j]), to, slot, (dp, to))

    def start_dispatch(i, carry):
        dispatch(lax.rem(expert + i, count), expert).start()
        return carry

    lax.fori_loop(1, count, start_dispatch, 0)
    for j in range(2):
        arr[c, j, expert] = outbox[j, expert]
    forward(expert).start()

    def pass_on(i, carry):
        source = lax.rem(expert + count - i, count)
        dispatch(source, source).wait_recv()
        forward(source).start()
        return carry

    lax.fori_loop(1, count, pass_on, 0)
    loads[L_GATE].wait()
    loads[L_UP].wait()

    def project(half, first):
        for j in range(2):
            rows = arr[half, j].reshape(count * slots, width)
            for total, weight in ((gate, wg), (up, wu)):
                value = jnp.dot(rows, weight[2 * half + j], preferred_element_type=F32)
                if first and j == 0:
                    total[...] = value
                else:
                    total[...] += value

    project(c, True)

    def arrived(source, carry):
        forward(source).wait_recv()
        return carry

    lax.fori_loop(0, count, arrived, 0)
    project(1 - c, False)
    gated = jnp.minimum(gate[...], LIMIT)
    lifted = jnp.clip(up[...], -LIMIT, LIMIT)
    activated = (gated * jax.nn.sigmoid(1.702 * gated) * (lifted + 1.0)).astype(BF16)
    loads[L_DOWN].wait()

    def down(k):
        return lax.dot_general(activated, wd[k], (((1,), (1,)), ((), ())), preferred_element_type=F32)

    pair_in = []
    for j in range(2):
        osend[j] = down(2 * (1 - c) + j).astype(BF16)
        pair_in.append(send(osend.at[j], orecv.at[j], S_OUT + j, S_OUT + j, 1))
    for j in range(2):
        own = down(2 * c + j)
        pair_in[j].wait_recv()
        rbuf[j] = (own + orecv[j].astype(F32)).astype(BF16).reshape(count, slots, width)

        def start_return(i, carry):
            giveback(j, lax.rem(expert + i, count), expert).start()
            return carry

        lax.fori_loop(1, count, start_return, 0)
        ret[j, expert] = rbuf[j, expert]

    high = share.astype(BF16)
    low = (share - high.astype(F32)).astype(BF16)
    both = jnp.concatenate([high, low], axis=0)
    group_rows = share.shape[0]
    for j in range(2):

        def returned(source, carry):
            @pl.when(source != expert)
            def _():
                giveback(j, source, source).wait_recv()

            return carry

        lax.fori_loop(0, count, returned, 0)
        mixed = jnp.dot(both, ret[j].reshape(count * slots, width), preferred_element_type=F32)
        part_s[j] = (mixed[:group_rows] + mixed[group_rows:]).astype(BF16)
    send(part_s, part_r, S_PART, S_PART, 2).wait_recv()
    for j in range(2):
        moe_out = part_s[j].astype(F32) + part_r[j].astype(F32)
        nextb[c, j] = (stream[2 * c + j] + moe_out).astype(BF16)
    next_in = send(nextb.at[c], nextb.at[c], S_NEXT, S_NEXT, 1)
    next_in.wait_recv()
    rows = [nextb[k // 2, k % 2].astype(F32) for k in range(NDP)]
    for k in range(NDP):
        nextf[k] = rows[k]
    loads[L_AGAIN].wait()
    inputs = normalized(rows, [again[:, width * k : width * k + width] for k in range(NDP)])
    loads[L_QKV].wait()
    qkv = sum(jnp.dot(inputs[k], wq[k], preferred_element_type=F32) for k in range(NDP))
    columns = qkv.shape[1]
    for d in range(NDP):
        qbuf[d] = qkv[ROWS * d : ROWS * d + ROWS].astype(BF16)
    own_columns = pl.ds(pl.multiple_of(dp * columns, 128), columns)
    qkv_in = []
    for offset in (2, 3, 1):
        peer = group_peer(z, c, offset)
        theirs = lax.rem(peer, 2) * 2 + lax.div(peer, 2)
        qkv_in.append(
            send(qbuf.at[theirs], qkv_out.at[:, own_columns], S_QKV + offset - 1, S_QKV + offset - 1, offset)
        )
    qkv_out[:, own_columns] = qbuf[block]
    start = pl.multiple_of(block * ROWS, ROWS)
    for k in range(NDP):
        next_out[:, width * k : width * k + width] = nextf[k, pl.ds(start, ROWS), :].astype(BF16)

    def all_sent(i, carry):
        to = lax.rem(expert + i, count)
        dispatch(to, expert).wait_send()
        for j in range(2):
            giveback(j, to, expert).wait_send()
        return carry

    lax.fori_loop(1, count, all_sent, 0)

    def all_passed(source, carry):
        forward(source).wait_send()
        return carry

    lax.fori_loop(0, count, all_passed, 0)
    for copy in sent:
        copy.wait_send()
    for copy in qkv_in:
        copy.wait_recv()


def layer_call(args, count):
    (queries, kv_pool, page_table, held_tokens, sinks, residual, route_ids, route_weights, moe_gain,
     w_gate, w_up, w_down, o_weight, attn_gain, qkv_weight) = args
    width = residual.shape[1] // NDP
    hidden = w_gate.shape[2]
    columns = qkv_weight.shape[1]
    slots = NDP * (2 * ROWS * TOP // count)
    group_rows = NDP * ROWS
    all_slots = count * slots
    hbm = pl.BlockSpec(memory_space=pltpu.HBM)
    out = pl.BlockSpec(memory_space=pltpu.VMEM)
    vmem, dma = pltpu.VMEM, pltpu.SemaphoreType.DMA
    pairs = (2, ROWS, HEADS // 2, PAIR)
    return pl.pallas_call(
        layer_kernel,
        out_shape=(
            jax.ShapeDtypeStruct((ROWS, NDP * width), BF16),
            jax.ShapeDtypeStruct((ROWS, NDP * columns), BF16),
        ),
        in_specs=[hbm] * 15,
        out_specs=(out, out),
        scratch_shapes=[
            vmem(kv_pool.shape, BF16),
            vmem((width, HEADS * HD), BF16),
            vmem((NDP, width, hidden), BF16),
            vmem((NDP, width, hidden), BF16),
            vmem((NDP, width, hidden), BF16),
            vmem((NDP, width, columns), BF16),
            pltpu.SMEM((NDP,) + page_table.shape, jnp.int32),
            pltpu.SMEM((NDP, NDP, ROWS), jnp.int32),
            pltpu.SMEM((TOP, ROWS), jnp.int32),
            pltpu.SMEM((TOP, ROWS), F32),
            vmem((1, HEADS), F32),
            vmem((1, NDP * width), F32),
            vmem((1, NDP * width), F32),
            vmem((NDP, ROWS, HEADS * HD), BF16),
            vmem((ROWS * HEADS // 2, PAIR), F32),
            vmem((NDP, ROWS, NDP * width), BF16),
            vmem((ROWS, all_slots), F32),
            vmem((NDP, ROWS, all_slots), F32),
            vmem(pairs, F32),
            vmem((2, HEADS, PAIR), F32),
            vmem(pairs, BF16),
            vmem((2, HEADS, PAIR), F32),
            vmem(pairs, BF16),
            vmem((2, HEADS, PAIR), F32),
            vmem(pairs, BF16),
            vmem((HEADS, PAIR), F32),
            vmem(pairs, BF16),
            vmem((HEADS, PAIR), F32),
            vmem((2 * ROWS * HEADS // 2, PAIR), F32),
            vmem((2, 2 * ROWS, HEADS * HD), BF16),
            vmem((NDP, group_rows, width), BF16),
            vmem((NDP, group_rows, width), F32),
            vmem((NDP, group_rows, width), BF16),
            vmem((2, count, slots, width), BF16),
            vmem((2, 2, count, slots, width), BF16),
            vmem((all_slots, hidden), F32),
            vmem((all_slots, hidden), F32),
            vmem((2, all_slots, width), BF16),
            vmem((2, all_slots, width), BF16),
            vmem((2, count, slots, width), BF16),
            vmem((2, count, slots, width), BF16),
            vmem((2, group_rows, width), BF16),
            vmem((2, group_rows, width), BF16),
            vmem((2, 2, group_rows, width), BF16),
            vmem((NDP, group_rows, width), F32),
            vmem((NDP, ROWS, columns), BF16),
            dma((15,)),
            dma((N_SEM,)),
            dma((N_SEM,)),
            dma((count,)),
            dma((count,)),
            dma((count,)),
            dma((count,)),
            dma((2, count)),
            dma((2, count)),
        ],
        compiler_params=pltpu.CompilerParams(collective_id=0, has_side_effects=True, vmem_limit_bytes=44 * 2**20),
        name="layer",
    )(
        queries,
        kv_pool,
        page_table,
        held_tokens.T,
        sinks.reshape(1, HEADS),
        residual,
        route_ids.T,
        route_weights.T,
        moe_gain.reshape(1, NDP * width),
        w_gate.reshape(NDP, width, hidden),
        w_up.reshape(NDP, width, hidden),
        w_down[0].T.reshape(NDP, width, hidden),
        o_weight.T,
        attn_gain.reshape(1, NDP * width),
        qkv_weight.reshape(NDP, width, columns),
    )


def body(*args):
    return layer_call(args, lax.axis_size("expert"))


def solution(mesh):
    in_specs = (
        P(("dp", "expert"), None),
        P(("dp", "expert"), None, None),
        P(("dp", "expert"), None, None),
        P(("dp", "expert"), None),
        P(),
        P(("dp", "expert"), None),
        P(("dp", "expert"), None),
        P(("dp", "expert"), None),
        P(),
        P("expert", None, "dp"),
        P("expert", None, "dp"),
        P("expert", "dp", None),
        P(None, "dp"),
        P(),
        P(None, "dp"),
    )
    out_specs = (P(("dp", "expert"), None), P(("dp", "expert"), None))
    return jax.shard_map(body, mesh=mesh, in_specs=in_specs, out_specs=out_specs, check_vma=False)
```

time: 91.7 us -> 90.9 us (level)
  other arithmetic: 3.1 us -> 0 us
  local copies, waits for them, and re-layouts: 10.6 us -> 12.6 us
    unnamed x12 -> x22, local copies, waits for them, and re-layouts: 5.8 us -> 11.2 us
    reshape x5 -> x2, local copies, waits for them, and re-layouts: 3.04 us -> 1.43 us  [the longest x1 0.72 us: layer_call(): moe_gain.reshape(1, NDP * width)]
    reduce_sum x3 -> x0, other arithmetic: 1.56 us -> none  [the longest x1 0.76 us: combine_table(): shares = jnp.sum(jnp.where(chosen, share[:, :, None], 0.0), axis=1)]
    broadcast_in_dim x5 -> x0, local copies, waits for them, and re-layouts: 1.13 us -> none  [the longest x1 0.77 us: attention_call(): held_tokens[:, :, None]]
    pallas_call x2 -> x1, Pallas kernels: 76.7 us -> 77.1 us  [layer_call(): pl.pallas_call(layer_kernel, out_shape=(jax.ShapeDtypeStruct((ROWS, NDP *...]
where the time goes in v3:
time: 90.9 us; the launch traced here: 90.3 us
  Pallas kernels  77.1 us (85%)
  local copies, waits for them, and re-layouts  12.6 us (14%)
    pallas_call x1, Pallas kernels, layer_call(): pl.pallas_call(layer_kernel, out_shape=(jax.ShapeDtypeStruct((ROWS, NDP *...  77.1 us
    unnamed x22, local copies, waits for them, and re-layouts  11.2 us

profile of v3, /device:TPU:1, one launch (start us, length us, event | category | flops | bytes accessed | tf_op | source)
XLA Modules:
  0.0 90.3 jit_solution(11189000186479024916)
XLA Ops:
  0.6 0.7 reshape.26.mgain_hbm
  1.3 0.7 reshape.30.again_hbm
  2.1 0.0 copy-start
  2.1 1.6 %copy-done = bf16[1,2880,384]{2,1,0:T(8,128)(2,1)S(1)} copy-done((bf16[1,2880,384]{2,1,0:T(8,128)(2,1)S(1)}, bf16[1,2880,384]{2,1,0:T(8,128)(2,1)}, u32[]{:S(2)}) %copy-start) | copy-done | bytes 2211864
  3.7 0.0 copy-start.1
  3.7 1.6 %copy-done.1 = bf16[1,2880,384]{2,1,0:T(8,128)(2,1)S(1)} copy-done((bf16[1,2880,384]{2,1,0:T(8,128)(2,1)S(1)}, bf16[1,2880,384]{2,1,0:T(8,128)(2,1)}, u32[]{:S(2)}) %copy-start.1) | copy-done | bytes 2211864
  5.3 0.0 copy-start.2
  5.3 1.6 %copy-done.2 = bf16[1,384,2880]{1,2,0:T(8,128)(2,1)S(1)} copy-done((bf16[1,384,2880]{1,2,0:T(8,128)(2,1)S(1)}, bf16[1,384,2880]{1,2,0:T(8,128)(2,1)}, u32[]{:S(2)}) %copy-start.2) | copy-done | bytes 2211864
  6.9 0.0 copy-start.3
  6.9 0.8 copy-done.3
  7.8 0.0 copy-start.4
  7.8 0.8 copy-done.4
  8.6 0.0 copy-start.5
  8.6 0.7 copy-done.5
  9.3 0.0 copy-start.6
  9.3 0.7 copy-done.6
  10.0 0.0 copy-start.7
  10.0 0.7 copy-done.7
  10.7 0.0 copy-start.8
  10.7 0.7 copy-done.8
  11.3 0.0 copy-start.9
  11.3 0.7 copy-done.9
  12.0 77.1 %layer.1 = (bf16[8,2880]{1,0:T(8,128)(2,1)S(1)}, bf16[8,5120]{1,0:T(8,128)(2,1)S(1)}) custom-call(bf16[8,4096]{1,0:T(8,128)(2,1)S(1)} %copy-done.3, bf16[128,16,1024]{2,1,0:T(8,128)(2,1)} %pool_hbm.1, s32[8,4,16]{2,1,0:T(4,128)S(1)} %copy-done.5, s32[4,8]{1,0:T(4,128)S(1)} %bitcast.16, f32[1,64]{1,0:T(1,128)S(1)} %bitcast.19, bf16[8,2880]{1,0:T(8,128)(2,1)S(1)} %copy-done.4, ...), custom_call_target="tpu_custom_call" | custom-call | tf_op jit(solution)/shard_map/layer/pallas_call | solution.py:497
  89.1 0.6 copy.19
  89.7 0.6 copy.20
Async XLA Ops:
  2.1 1.6 %copy-start = (bf16[1,2880,384]{2,1,0:T(8,128)(2,1)S(1)}, bf16[1,2880,384]{2,1,0:T(8,128)(2,1)}, u32[]{:S(2)}) copy-start(bf16[1,2880,384]{2,1,0:T(8,128)(2,1)} %param.24) | copy-start | bytes 6635524
  3.7 1.6 %copy-start.1 = (bf16[1,2880,384]{2,1,0:T(8,128)(2,1)S(1)}, bf16[1,2880,384]{2,1,0:T(8,128)(2,1)}, u32[]{:S(2)}) copy-start(bf16[1,2880,384]{2,1,0:T(8,128)(2,1)} %param.25) | copy-start | bytes 6635524
  5.3 1.6 %copy-start.2 = (bf16[1,384,2880]{1,2,0:T(8,128)(2,1)S(1)}, bf16[1,384,2880]{1,2,0:T(8,128)(2,1)}, u32[]{:S(2)}) copy-start(bf16[1,384,2880]{1,2,0:T(8,128)(2,1)} %param.26) | copy-start | bytes 6635524
  6.9 0.8 copy-start.3
  7.8 0.8 copy-start.4
  8.6 0.7 copy-start.5
  9.3 0.7 copy-start.6
  10.0 0.7 copy-start.7
  10.7 0.7 copy-start.8
  11.3 0.7 copy-start.9

commit v4 on v3

--- a/solution.py
+++ b/solution.py
@@ -25,9 +25,9 @@
 F32 = jnp.float32
 BF16 = jnp.bfloat16
 
-S_TAB, S_HELD, S_Q, S_RES, S_COM, S_PAIR_N, S_PAIR_ML, S_X_N, S_X_ML, S_LHS, S_PROJ = 0, 3, 6, 9, 12, 15, 17, 19, 21, 22, 23
-S_OUT, S_PART, S_NEXT, S_QKV = 26, 28, 29, 30
-N_SEM = 33
+S_TAB, S_HELD, S_Q, S_RES, S_COM, S_SUM, S_QKV = range(0, 21, 3)
+S_PAIR_N, S_PAIR_ML, S_X_N, S_OUT, S_PART, S_NEXT = range(21, 33, 2)
+S_X_ML, S_LHS, S_STREAM, N_SEM = range(33, 37)
 L_TAB, L_HELD, L_Q, L_POOL, L_SINK, L_IDS, L_WEIGHTS, L_RES, L_OW, L_MGAIN, L_GATE, L_UP, L_DOWN, L_AGAIN, L_QKV = range(15)
 
 
@@ -86,13 +86,6 @@
 def pair_columns(column):
     lane = lax.broadcasted_iota(jnp.int32, (HEADS // 2, PAIR), 1)
     return jnp.where(lane < HD, column[: HEADS // 2], column[HEADS // 2 :])
-
-
-def normalized(blocks, gains):
-    total = sum(jnp.sum(block * block, axis=1, keepdims=True) for block in blocks)
-    width = sum(block.shape[1] for block in blocks)
-    scale = lax.rsqrt(total / width + EPSILON)
-    return [(block * scale * gain).astype(BF16) for block, gain in zip(blocks, gains)]
 
 
 def attend(queries, tables, counts, holder, pool, rows, write):
@@ -157,9 +150,9 @@
     wg_hbm, wu_hbm, wd_hbm, ow_hbm, again_hbm, wq_hbm,
     next_out, qkv_out,
     pool, ow, wg, wu, wd, wq,
-    tabs, helds, ids, weights, sinks, mgain, again, qraw, qwide, resraw, comown, comall,
-    keep_n, keep_ml, send_n, send_ml, recv_n, recv_ml, xs_n, xs_ml, xr_n, xr_ml, att, lhs, pall, stream,
-    xin, outbox, arr, gate, up, osend, orecv, rbuf, ret, part_s, part_r, nextb, nextf, qbuf,
+    tabs, helds, ids, weights, sinks, mgain, again, gains, qraw, qwide, resraw, resblk, resall, comown, comall,
+    keep_n, keep_ml, send_n, send_ml, recv_n, recv_ml, xs_n, xs_ml, xr_n, xr_ml, att, lhs, stream, sums,
+    outbox, arr, gate, up, osend, orecv, rbuf, ret, part_s, part_r, nextb, nextf, qbuf,
     load_sem, send_sem, recv_sem, d_send, d_recv, f_send, f_recv, r_send, r_recv,
 ):
     dp, z, c, expert = position()
@@ -182,16 +175,16 @@
         (L_HELD, held_hbm, helds.at[dp]),
         (L_Q, q_hbm, qraw.at[dp]),
         (L_POOL, pool_hbm, pool),
-        (L_SINK, sink_hbm, sinks),
         (L_IDS, ids_hbm, ids),
         (L_WEIGHTS, weights_hbm, weights),
-        (L_RES, res_hbm, resraw.at[block]),
+        (L_RES, res_hbm, resraw),
+        (L_MGAIN, mgain_hbm, mgain),
+        (L_AGAIN, again_hbm, again),
+        (L_SINK, sink_hbm, sinks),
         (L_OW, ow_hbm, ow),
-        (L_MGAIN, mgain_hbm, mgain),
         (L_GATE, wg_hbm, wg),
         (L_UP, wu_hbm, wu),
         (L_DOWN, wd_hbm, wd),
-        (L_AGAIN, again_hbm, again),
         (L_QKV, wq_hbm, wq),
     ):
         loads[number] = pltpu.make_async_copy(src, dst, load_sem.at[number])
@@ -261,31 +254,41 @@
             xs_n[number, row] = merged.astype(BF16)
         return send(xs_n.at[number], xr_n.at[1 - number], S_X_N + number, S_X_N + 1 - number, 2)
 
+    for number in (L_IDS, L_WEIGHTS, L_RES, L_MGAIN, L_AGAIN):
+        loads[number].wait()
+    combine_rows(ids, weights, comown, block, slots)
+    comall[block] = comown[...]
+    for which, gain in enumerate((mgain, again)):
+        whole = gain[...].reshape(1, NDP * width)
+        for k in range(NDP):
+            gains[which, k] = whole[:, width * k : width * k + width]
+    for k in range(NDP):
+        resblk[k] = resraw[:, width * k : width * k + width]
+    resall[block] = resblk[dp]
+    for number in (L_TAB, L_HELD, L_Q, L_POOL):
+        loads[number].wait()
+    run_block(0, 0, keep_n, keep_ml)
+
     pl.semaphore_wait(barrier, count + 2)
+    for offset in (2, 1):
+        q_in[offset] = send(q_hbm, qraw.at[dp], S_Q + offset - 1, S_Q + offset - 1, offset)
     for offset in (2, 3, 1):
         tab_in[offset] = send(tab_hbm, tabs.at[dp], S_TAB + offset - 1, S_TAB + offset - 1, offset)
         held_in[offset] = send(held_hbm, helds.at[dp], S_HELD + offset - 1, S_HELD + offset - 1, offset)
-        q_in[offset] = send(q_hbm, qraw.at[dp], S_Q + offset - 1, S_Q + offset - 1, offset)
     for offset in (2, 3, 1):
-        res_in[offset] = send(res_hbm, resraw.at[block], S_RES + offset - 1, S_RES + offset - 1, offset)
-    for number in (L_IDS, L_WEIGHTS):
-        loads[number].wait()
-    combine_rows(ids, weights, comown, block, slots)
-    comall[block] = comown[...]
-    for offset in (2, 3, 1):
+        peer = group_peer(z, c, offset)
+        res_in[offset] = send(resblk.at[peer], resall.at[block], S_RES + offset - 1, S_RES + offset - 1, offset)
         com_in[offset] = send(comown, comall.at[block], S_COM + offset - 1, S_COM + offset - 1, offset)
-
-    for number in (L_TAB, L_HELD, L_Q, L_POOL):
-        loads[number].wait()
-    run_block(0, 0, keep_n, keep_ml)
     fetch_block(1)
     run_block(1, 0, send_n, send_ml)
     pair_in = [send_pair(0)]
+    fetch_block(2)
+    cross = group_peer(z, c, 2)
+    q_in[3] = send(qraw.at[cross], qraw.at[cross], S_Q + 2, S_Q + 2, 1)
+    cross_in = [merge_pair(0, pair_in[0])]
     fetch_block(3)
     run_block(3, 1, send_n, send_ml)
     pair_in.append(send_pair(1))
-    cross_in = [merge_pair(0, pair_in[0])]
-    fetch_block(2)
     run_block(2, 1, keep_n, keep_ml)
     cross_in.append(merge_pair(1, pair_in[1]))
     xs_ml[...] = keep_ml[0] + keep_ml[1]
@@ -316,31 +319,27 @@
     lhs_in.wait_recv()
     rows = jnp.concatenate([lhs[0], lhs[1]], axis=0)
     projected = lax.dot_general(rows, ow[...], (((1,), (1,)), ((), ())), preferred_element_type=F32)
-    pall[dp] = projected.astype(BF16)
-    proj_in = [
-        send(pall.at[dp], pall.at[dp], S_PROJ + offset - 1, S_PROJ + offset - 1, offset) for offset in (2, 3, 1)
+    for offset in (1, 2, 3):
+        res_in[offset].wait_recv()
+    residual = jnp.concatenate([resall[d].astype(F32) for d in range(NDP)], axis=0)
+    stream[z] = (residual + projected.astype(BF16).astype(F32)).astype(BF16)
+    stream_in = send(stream.at[z], stream.at[z], S_STREAM, S_STREAM, 2)
+    own = stream[z].astype(F32)
+    sums[dp] = jnp.broadcast_to(jnp.sum(own * own, axis=1, keepdims=True), sums.shape[1:])
+    sum_in = [
+        send(sums.at[dp], sums.at[dp], S_SUM + offset - 1, S_SUM + offset - 1, offset) for offset in (2, 3, 1)
     ]
     for offset in (1, 2, 3):
-        res_in[offset].wait_recv()
         com_in[offset].wait_recv()
-    for copy in proj_in:
-        copy.wait_recv()
-    loads[L_RES].wait()
-    loads[L_MGAIN].wait()
-    rows = []
-    for k in range(NDP):
-        residual = jnp.concatenate(
-            [resraw[d, :, width * k : width * k + width].astype(F32) for d in range(NDP)], axis=0
-        )
-        rows.append((residual + pall[k].astype(F32)).astype(BF16).astype(F32))
-        stream[k] = rows[k]
-    gains = [mgain[:, width * k : width * k + width] for k in range(NDP)]
-    for k, value in enumerate(normalized(rows, gains)):
-        xin[k] = value
     share = jnp.concatenate([comall[d] for d in range(NDP)], axis=0)
     picks = (share > 0).astype(F32).T.astype(BF16)
+    for copy in sum_in:
+        copy.wait_recv()
+    scale = lax.rsqrt((sums[0] + sums[1] + sums[2] + sums[3]) / (NDP * width) + EPSILON)[:, :1]
+    stream_in.wait_recv()
     for j in range(2):
-        picked = jnp.dot(picks, xin[2 * c + j], preferred_element_type=F32).astype(BF16)
+        rows = (stream[j].astype(F32) * scale * gains[0, 2 * j + c]).astype(BF16)
+        picked = jnp.dot(picks, rows, preferred_element_type=F32).astype(BF16)
         outbox[j] = picked.reshape(count, slots, width)
 
     def dispatch(to, slot):
@@ -378,7 +377,7 @@
         for j in range(2):
             rows = arr[half, j].reshape(count * slots, width)
             for total, weight in ((gate, wg), (up, wu)):
-                value = jnp.dot(rows, weight[2 * half + j], preferred_element_type=F32)
+                value = jnp.dot(rows, weight[2 * j + half], preferred_element_type=F32)
                 if first and j == 0:
                     total[...] = value
                 else:
@@ -402,10 +401,10 @@
 
     pair_in = []
     for j in range(2):
-        osend[j] = down(2 * (1 - c) + j).astype(BF16)
+        osend[j] = down(2 * j + 1 - c).astype(BF16)
         pair_in.append(send(osend.at[j], orecv.at[j], S_OUT + j, S_OUT + j, 1))
     for j in range(2):
-        own = down(2 * c + j)
+        own = down(2 * j + c)
         pair_in[j].wait_recv()
         rbuf[j] = (own + orecv[j].astype(F32)).astype(BF16).reshape(count, slots, width)
 
@@ -420,6 +419,7 @@
     low = (share - high.astype(F32)).astype(BF16)
     both = jnp.concatenate([high, low], axis=0)
     group_rows = share.shape[0]
+    part_in = []
     for j in range(2):
 
         def returned(source, carry):
@@ -432,19 +432,30 @@
         lax.fori_loop(0, count, returned, 0)
         mixed = jnp.dot(both, ret[j].reshape(count * slots, width), preferred_element_type=F32)
         part_s[j] = (mixed[:group_rows] + mixed[group_rows:]).astype(BF16)
-    send(part_s, part_r, S_PART, S_PART, 2).wait_recv()
+        part_in.append(send(part_s.at[j], part_r.at[j], S_PART + j, S_PART + j, 2))
+    loads[L_QKV].wait()
+    next_in = []
+    qkv = jnp.zeros((group_rows, wq.shape[2]), F32)
+    squares = jnp.zeros((group_rows, 1), F32)
+
+    def project_next(half, j, qkv, squares):
+        k = 2 * j + half
+        rows = nextb[half, j].astype(F32)
+        nextf[k] = rows
+        squares += jnp.sum(rows * rows, axis=1, keepdims=True)
+        qkv += jnp.dot((rows * gains[1, k]).astype(BF16), wq[k], preferred_element_type=F32)
+        return qkv, squares
+
     for j in range(2):
+        part_in[j].wait_recv()
         moe_out = part_s[j].astype(F32) + part_r[j].astype(F32)
-        nextb[c, j] = (stream[2 * c + j] + moe_out).astype(BF16)
-    next_in = send(nextb.at[c], nextb.at[c], S_NEXT, S_NEXT, 1)
-    next_in.wait_recv()
-    rows = [nextb[k // 2, k % 2].astype(F32) for k in range(NDP)]
-    for k in range(NDP):
-        nextf[k] = rows[k]
-    loads[L_AGAIN].wait()
-    inputs = normalized(rows, [again[:, width * k : width * k + width] for k in range(NDP)])
-    loads[L_QKV].wait()
-    qkv = sum(jnp.dot(inputs[k], wq[k], preferred_element_type=F32) for k in range(NDP))
+        nextb[c, j] = (stream[j].astype(F32) + moe_out).astype(BF16)
+        next_in.append(send(nextb.at[c, j], nextb.at[c, j], S_NEXT + j, S_NEXT + j, 1))
+        qkv, squares = project_next(c, j, qkv, squares)
+    for j in range(2):
+        next_in[j].wait_recv()
+        qkv, squares = project_next(1 - c, j, qkv, squares)
+    qkv = qkv * lax.rsqrt(squares / (NDP * width) + EPSILON)
     columns = qkv.shape[1]
     for d in range(NDP):
         qbuf[d] = qkv[ROWS * d : ROWS * d + ROWS].astype(BF16)
@@ -514,11 +525,14 @@
             pltpu.SMEM((TOP, ROWS), jnp.int32),
             pltpu.SMEM((TOP, ROWS), F32),
             vmem((1, HEADS), F32),
-            vmem((1, NDP * width), F32),
-            vmem((1, NDP * width), F32),
+            vmem((NDP * width,), F32),
+            vmem((NDP * width,), F32),
+            vmem((2, NDP, 1, width), F32),
             vmem((NDP, ROWS, HEADS * HD), BF16),
             vmem((ROWS * HEADS // 2, PAIR), F32),
-            vmem((NDP, ROWS, NDP * width), BF16),
+            vmem((ROWS, NDP * width), BF16),
+            vmem((NDP, ROWS, width), BF16),
+            vmem((NDP, ROWS, width), BF16),
             vmem((ROWS, all_slots), F32),
             vmem((NDP, ROWS, all_slots), F32),
             vmem(pairs, F32),
@@ -533,9 +547,8 @@
             vmem((HEADS, PAIR), F32),
             vmem((2 * ROWS * HEADS // 2, PAIR), F32),
             vmem((2, 2 * ROWS, HEADS * HD), BF16),
-            vmem((NDP, group_rows, width), BF16),
-            vmem((NDP, group_rows, width), F32),
-            vmem((NDP, group_rows, width), BF16),
+            vmem((2, group_rows, width), BF16),
+            vmem((NDP, group_rows, 128), F32),
             vmem((2, count, slots, width), BF16),
             vmem((2, 2, count, slots, width), BF16),
             vmem((all_slots, hidden), F32),
@@ -561,7 +574,7 @@
         ],
         compiler_params=pltpu.CompilerParams(collective_id=0, has_side_effects=True, vmem_limit_bytes=44 * 2**20),
         name="layer",
-    )(
+    )(*[pltpu.with_memory_space_constraint(x, pltpu.HBM) for x in (
         queries,
         kv_pool,
         page_table,
@@ -570,14 +583,14 @@
         residual,
         route_ids.T,
         route_weights.T,
-        moe_gain.reshape(1, NDP * width),
+        moe_gain,
         w_gate.reshape(NDP, width, hidden),
         w_up.reshape(NDP, width, hidden),
         w_down[0].T.reshape(NDP, width, hidden),
         o_weight.T,
-        attn_gain.reshape(1, NDP * width),
+        attn_gain,
         qkv_weight.reshape(NDP, width, columns),
-    )
+    )])
 
 
 def body(*args):

time: 90.9 us -> 78.1 us (0.86)
  local copies, waits for them, and re-layouts: 12.6 us -> 1.26 us
  Pallas kernels: 77.1 us -> 76.1 us
    unnamed x22 -> x2, local copies, waits for them, and re-layouts: 11.2 us -> 1.26 us
    reshape x2 -> x0, local copies, waits for them, and re-layouts: 1.43 us -> none  [the longest x1 0.72 us: layer_call(): moe_gain.reshape(1, NDP * width)]
    pallas_call x1, Pallas kernels: 77.1 us -> 76.1 us  [layer_call(): pl.pallas_call(layer_kernel, out_shape=(jax.ShapeDtypeStruct((ROWS, NDP *...]
where the time goes in v4:
time: 78.1 us; the launch traced here: 78 us
  Pallas kernels  76.1 us (97%)
  local copies, waits for them, and re-layouts  1.26 us (2%)
    pallas_call x1, Pallas kernels, layer_call(): pl.pallas_call(layer_kernel, out_shape=(jax.ShapeDtypeStruct((ROWS, NDP *...  76.1 us

profile of v4, /device:TPU:1, one launch (start us, length us, event | category | flops | bytes accessed | tf_op | source)
XLA Modules:
  0.0 78.0 jit_solution(15462394132682782964)
XLA Ops:
  0.6 76.1 %layer.1 = (bf16[8,2880]{1,0:T(8,128)(2,1)S(1)}, bf16[8,5120]{1,0:T(8,128)(2,1)S(1)}) custom-call(bf16[8,4096]{1,0:T(8,128)(2,1)} %q_hbm.1, bf16[128,16,1024]{2,1,0:T(8,128)(2,1)} %pool_hbm.1, s32[8,4,16]{2,1,0:T(4,128)} %tab_hbm.1, s32[4,8]{1,0:T(4,128)} %bitcast.18, f32[1,64]{1,0:T(1,128)} %bitcast.21, bf16[8,2880]{1,0:T(8,128)(2,1)} %res_hbm.1, ...), custom_call_target="tpu_custom_call" | custom-call | tf_op jit(solution)/shard_map/layer/pallas_call | solution.py:508
  76.8 0.6 copy.19
  77.4 0.6 copy.20

commit v5 on v4

--- a/solution.py
+++ b/solution.py
@@ -26,8 +26,8 @@
 BF16 = jnp.bfloat16
 
 S_TAB, S_HELD, S_Q, S_RES, S_COM, S_SUM, S_QKV = range(0, 21, 3)
-S_PAIR_N, S_PAIR_ML, S_X_N, S_OUT, S_PART, S_NEXT = range(21, 33, 2)
-S_X_ML, S_LHS, S_STREAM, N_SEM = range(33, 37)
+S_PAIR_N, S_PAIR_ML, S_X_N, S_PART, S_NEXT = range(21, 31, 2)
+S_X_ML, S_LHS, S_STREAM, S_OUT, N_SEM = 31, 32, 33, 34, 38
 L_TAB, L_HELD, L_Q, L_POOL, L_SINK, L_IDS, L_WEIGHTS, L_RES, L_OW, L_MGAIN, L_GATE, L_UP, L_DOWN, L_AGAIN, L_QKV = range(15)
 
 
@@ -152,7 +152,7 @@
     pool, ow, wg, wu, wd, wq,
     tabs, helds, ids, weights, sinks, mgain, again, gains, qraw, qwide, resraw, resblk, resall, comown, comall,
     keep_n, keep_ml, send_n, send_ml, recv_n, recv_ml, xs_n, xs_ml, xr_n, xr_ml, att, lhs, stream, sums,
-    outbox, arr, gate, up, osend, orecv, rbuf, ret, part_s, part_r, nextb, nextf, qbuf,
+    outbox, arr, gate, up, osend, orecv, kept, rbuf, ret, part_s, part_r, nextb, nextf, qbuf,
     load_sem, send_sem, recv_sem, d_send, d_recv, f_send, f_recv, r_send, r_recv,
 ):
     dp, z, c, expert = position()
@@ -325,7 +325,14 @@
     stream[z] = (residual + projected.astype(BF16).astype(F32)).astype(BF16)
     stream_in = send(stream.at[z], stream.at[z], S_STREAM, S_STREAM, 2)
     own = stream[z].astype(F32)
-    sums[dp] = jnp.broadcast_to(jnp.sum(own * own, axis=1, keepdims=True), sums.shape[1:])
+    group_rows = own.shape[0]
+    diagonal = lax.broadcasted_iota(jnp.int32, (group_rows, 128), 0) == lax.broadcasted_iota(
+        jnp.int32, (group_rows, 128), 1
+    )
+    square = jnp.sum(own * own, axis=1, keepdims=True)
+    sums[dp] = jnp.broadcast_to(
+        jnp.sum(jnp.where(diagonal, square, 0.0), axis=0, keepdims=True), sums.shape[1:]
+    )
     sum_in = [
         send(sums.at[dp], sums.at[dp], S_SUM + offset - 1, S_SUM + offset - 1, offset) for offset in (2, 3, 1)
     ]
@@ -335,47 +342,56 @@
     picks = (share > 0).astype(F32).T.astype(BF16)
     for copy in sum_in:
         copy.wait_recv()
-    scale = lax.rsqrt((sums[0] + sums[1] + sums[2] + sums[3]) / (NDP * width) + EPSILON)[:, :1]
+    square = (sums[0] + sums[1] + sums[2] + sums[3])[:1]
+    square = jnp.sum(jnp.where(diagonal, square, 0.0), axis=1, keepdims=True)
+    scale = lax.rsqrt(square / (NDP * width) + EPSILON)
     stream_in.wait_recv()
     for j in range(2):
         rows = (stream[j].astype(F32) * scale * gains[0, 2 * j + c]).astype(BF16)
         picked = jnp.dot(picks, rows, preferred_element_type=F32).astype(BF16)
         outbox[j] = picked.reshape(count, slots, width)
 
-    def dispatch(to, slot):
-        return remote(outbox.at[:, to], arr.at[c, :, slot], (d_send, d_recv), to, slot, (dp, to))
-
-    def forward(source):
+    def partner(place, sign):
+        dy = 2 * lax.rem(lax.div(place, 8), 2) + lax.div(place, 16)
+        dz, dx = lax.rem(lax.div(place, 4), 2), lax.rem(place, 4)
+        at_z = lax.rem(lax.div(expert, 16) + dz, 2)
+        at_y = lax.rem(lax.rem(lax.div(expert, 4), 4) + sign * dy + 4, 4)
+        at_x = lax.rem(lax.rem(expert, 4) + sign * dx + 4, 4)
+        return 16 * at_z + 4 * at_y + at_x
+
+    def dispatch(place):
+        to = partner(place, 1)
+        return remote(outbox.at[:, to], arr.at[c, :, place], (d_send, d_recv), place, place, (dp, to))
+
+    def forward(place):
         return remote(
-            arr.at[c, :, source], arr.at[c, :, source], (f_send, f_recv), source, source,
+            arr.at[c, :, place], arr.at[c, :, place], (f_send, f_recv), place, place,
             (group_peer(z, c, 1), expert),
         )
 
-    def giveback(j, to, slot):
-        return remote(rbuf.at[j, to], ret.at[j, slot], (r_send.at[j], r_recv.at[j]), to, slot, (dp, to))
-
-    def start_dispatch(i, carry):
-        dispatch(lax.rem(expert + i, count), expert).start()
-        return carry
-
-    lax.fori_loop(1, count, start_dispatch, 0)
-    for j in range(2):
-        arr[c, j, expert] = outbox[j, expert]
-    forward(expert).start()
-
-    def pass_on(i, carry):
-        source = lax.rem(expert + count - i, count)
-        dispatch(source, source).wait_recv()
-        forward(source).start()
-        return carry
-
-    lax.fori_loop(1, count, pass_on, 0)
-    loads[L_GATE].wait()
-    loads[L_UP].wait()
-
-    def project(half, first):
+    def giveback(j, place):
+        to = partner(place, -1)
+        return remote(
+            rbuf.at[j, place], ret.at[j, expert], (r_send.at[j], r_recv.at[j]), place, place, (dp, to)
+        )
+
+    def each(first, last, act):
+        def step(place, carry):
+            act(place)
+            return carry
+
+        lax.fori_loop(first, last, step, 0)
+
+    batch = count // 2
+    batch_rows = batch * slots
+
+    def pass_on(place):
+        dispatch(place).wait_recv()
+        forward(place).start()
+
+    def project(first_place, half, first):
         for j in range(2):
-            rows = arr[half, j].reshape(count * slots, width)
+            rows = arr[half, j, first_place : first_place + batch].reshape(batch_rows, width)
             for total, weight in ((gate, wg), (up, wu)):
                 value = jnp.dot(rows, weight[2 * j + half], preferred_element_type=F32)
                 if first and j == 0:
@@ -383,53 +399,56 @@
                 else:
                     total[...] += value
 
-    project(c, True)
-
-    def arrived(source, carry):
-        forward(source).wait_recv()
-        return carry
-
-    lax.fori_loop(0, count, arrived, 0)
-    project(1 - c, False)
-    gated = jnp.minimum(gate[...], LIMIT)
-    lifted = jnp.clip(up[...], -LIMIT, LIMIT)
-    activated = (gated * jax.nn.sigmoid(1.702 * gated) * (lifted + 1.0)).astype(BF16)
-    loads[L_DOWN].wait()
-
-    def down(k):
-        return lax.dot_general(activated, wd[k], (((1,), (1,)), ((), ())), preferred_element_type=F32)
-
-    pair_in = []
+    def apply_experts(number):
+        first_place = number * batch
+        project(first_place, c, True)
+        each(first_place, first_place + batch, lambda place: forward(place).wait_recv())
+        project(first_place, 1 - c, False)
+        gated = jnp.minimum(gate[...], LIMIT)
+        lifted = jnp.clip(up[...], -LIMIT, LIMIT)
+        activated = (gated * jax.nn.sigmoid(1.702 * gated) * (lifted + 1.0)).astype(BF16)
+
+        def down(k):
+            return lax.dot_general(activated, wd[k], (((1,), (1,)), ((), ())), preferred_element_type=F32)
+
+        incoming = []
+        for j in range(2):
+            osend[number, j] = down(2 * j + 1 - c).astype(BF16)
+            at = S_OUT + 2 * number + j
+            incoming.append(send(osend.at[number, j], orecv.at[number, j], at, at, 1))
+        for j in range(2):
+            kept[j] = down(2 * j + c)
+        return incoming
+
+    def give_back(number, incoming):
+        first_place = number * batch
+        for j in range(2):
+            incoming[j].wait_recv()
+            total = (kept[j] + orecv[number, j].astype(F32)).astype(BF16)
+            rbuf[j, first_place : first_place + batch] = total.reshape(batch, slots, width)
+            each(max(first_place, 1), first_place + batch, lambda place: giveback(j, place).start())
+
+    each(1, count, lambda place: dispatch(place).start())
     for j in range(2):
-        osend[j] = down(2 * j + 1 - c).astype(BF16)
-        pair_in.append(send(osend.at[j], orecv.at[j], S_OUT + j, S_OUT + j, 1))
+        arr[c, j, 0] = outbox[j, expert]
+    forward(0).start()
+    each(1, batch, pass_on)
+    for number in (L_GATE, L_UP, L_DOWN):
+        loads[number].wait()
+    incoming = apply_experts(0)
+    each(batch, count, pass_on)
+    give_back(0, incoming)
+    incoming = apply_experts(1)
+    give_back(1, incoming)
     for j in range(2):
-        own = down(2 * j + c)
-        pair_in[j].wait_recv()
-        rbuf[j] = (own + orecv[j].astype(F32)).astype(BF16).reshape(count, slots, width)
-
-        def start_return(i, carry):
-            giveback(j, lax.rem(expert + i, count), expert).start()
-            return carry
-
-        lax.fori_loop(1, count, start_return, 0)
-        ret[j, expert] = rbuf[j, expert]
+        ret[j, expert] = rbuf[j, 0]
 
     high = share.astype(BF16)
     low = (share - high.astype(F32)).astype(BF16)
     both = jnp.concatenate([high, low], axis=0)
-    group_rows = share.shape[0]
     part_in = []
     for j in range(2):
-
-        def returned(source, carry):
-            @pl.when(source != expert)
-            def _():
-                giveback(j, source, source).wait_recv()
-
-            return carry
-
-        lax.fori_loop(0, count, returned, 0)
+        each(1, count, lambda place: giveback(j, place).wait_recv())
         mixed = jnp.dot(both, ret[j].reshape(count * slots, width), preferred_element_type=F32)
         part_s[j] = (mixed[:group_rows] + mixed[group_rows:]).astype(BF16)
         part_in.append(send(part_s.at[j], part_r.at[j], S_PART + j, S_PART + j, 2))
@@ -472,20 +491,13 @@
     for k in range(NDP):
         next_out[:, width * k : width * k + width] = nextf[k, pl.ds(start, ROWS), :].astype(BF16)
 
-    def all_sent(i, carry):
-        to = lax.rem(expert + i, count)
-        dispatch(to, expert).wait_send()
+    def all_sent(place):
+        dispatch(place).wait_send()
         for j in range(2):
-            giveback(j, to, expert).wait_send()
-        return carry
-
-    lax.fori_loop(1, count, all_sent, 0)
-
-    def all_passed(source, carry):
-        forward(source).wait_send()
-        return carry
-
-    lax.fori_loop(0, count, all_passed, 0)
+            giveback(j, place).wait_send()
+
+    each(1, count, all_sent)
+    each(0, count, lambda place: forward(place).wait_send())
     for copy in sent:
         copy.wait_send()
     for copy in qkv_in:
@@ -548,13 +560,14 @@
             vmem((2 * ROWS * HEADS // 2, PAIR), F32),
             vmem((2, 2 * ROWS, HEADS * HD), BF16),
             vmem((2, group_rows, width), BF16),
-            vmem((NDP, group_rows, 128), F32),
+            vmem((NDP, 8, 128), F32),
             vmem((2, count, slots, width), BF16),
             vmem((2, 2, count, slots, width), BF16),
-            vmem((all_slots, hidden), F32),
-            vmem((all_slots, hidden), F32),
-            vmem((2, all_slots, width), BF16),
-            vmem((2, all_slots, width), BF16),
+            vmem((all_slots // 2, hidden), F32),
+            vmem((all_slots // 2, hidden), F32),
+            vmem((2, 2, all_slots // 2, width), BF16),
+            vmem((2, 2, all_slots // 2, width), BF16),
+            vmem((2, all_slots // 2, width), F32),
             vmem((2, count, slots, width), BF16),
             vmem((2, count, slots, width), BF16),
             vmem((2, group_rows, width), BF16),

time: 78.1 us -> 74.7 us (0.956)
  Pallas kernels: 76.1 us -> 72.6 us
    pallas_call x1, Pallas kernels: 76.1 us -> 72.6 us  [layer_call(): pl.pallas_call(layer_kernel, out_shape=(jax.ShapeDtypeStruct((ROWS, NDP *...]
where the time goes in v5:
time: 74.7 us; the launch traced here: 74.5 us
  Pallas kernels  72.6 us (97%)
  local copies, waits for them, and re-layouts  1.26 us (2%)
    pallas_call x1, Pallas kernels, layer_call(): pl.pallas_call(layer_kernel, out_shape=(jax.ShapeDtypeStruct((ROWS, NDP *...  72.6 us

profile of v5, /device:TPU:1, one launch (start us, length us, event | category | flops | bytes accessed | tf_op | source)
XLA Modules:
  0.0 74.5 jit_solution(12032949068576783754)
XLA Ops:
  0.6 72.6 %layer.1 = (bf16[8,2880]{1,0:T(8,128)(2,1)S(1)}, bf16[8,5120]{1,0:T(8,128)(2,1)S(1)}) custom-call(bf16[8,4096]{1,0:T(8,128)(2,1)} %q_hbm.1, bf16[128,16,1024]{2,1,0:T(8,128)(2,1)} %pool_hbm.1, s32[8,4,16]{2,1,0:T(4,128)} %tab_hbm.1, s32[4,8]{1,0:T(4,128)} %bitcast.18, f32[1,64]{1,0:T(1,128)} %bitcast.21, bf16[8,2880]{1,0:T(8,128)(2,1)} %res_hbm.1, ...), custom_call_target="tpu_custom_call" | custom-call | tf_op jit(solution)/shard_map/layer/pallas_call | solution.py:520
  73.3 0.6 copy.19
  73.9 0.6 copy.20

commit v6 on v5

--- a/solution.py
+++ b/solution.py
@@ -153,7 +153,7 @@
     tabs, helds, ids, weights, sinks, mgain, again, gains, qraw, qwide, resraw, resblk, resall, comown, comall,
     keep_n, keep_ml, send_n, send_ml, recv_n, recv_ml, xs_n, xs_ml, xr_n, xr_ml, att, lhs, stream, sums,
     outbox, arr, gate, up, osend, orecv, kept, rbuf, ret, part_s, part_r, nextb, nextf, qbuf,
-    load_sem, send_sem, recv_sem, d_send, d_recv, f_send, f_recv, r_send, r_recv,
+    load_sem, send_sem, recv_sem, d_send, d_recv, f_send, f_recv, r_send, r_recv, round_sem,
 ):
     dp, z, c, expert = position()
     sems = (send_sem, recv_sem)
@@ -164,11 +164,18 @@
     for offset in (1, 2, 3):
         pl.semaphore_signal(barrier, inc=1, device_id=(group_peer(z, c, offset), expert), device_id_type=MESH)
 
-    def greet(i, carry):
-        pl.semaphore_signal(barrier, inc=1, device_id=(dp, lax.rem(expert + i, count)), device_id_type=MESH)
-        return carry
-
-    lax.fori_loop(1, count, greet, 0)
+    def neighbour(digit):
+        step = 1 << digit
+        return (dp, expert + step * (1 - 2 * lax.rem(lax.div(expert, step), 2)))
+
+    digits = count.bit_length() - 1
+    for digit in range(digits):
+        pl.semaphore_signal(barrier, inc=1, device_id=neighbour(digit), device_id_type=MESH)
+
+    def know(digit):
+        pl.semaphore_signal(round_sem.at[digit], inc=1, device_id=neighbour(digit), device_id_type=MESH)
+        pl.semaphore_wait(round_sem.at[digit], 1)
+
     loads = {}
     for number, src, dst in (
         (L_TAB, tab_hbm, tabs.at[dp]),
@@ -254,6 +261,20 @@
             xs_n[number, row] = merged.astype(BF16)
         return send(xs_n.at[number], xr_n.at[1 - number], S_X_N + number, S_X_N + 1 - number, 2)
 
+    pl.semaphore_wait(barrier, 3 + digits)
+    for offset in (2, 1):
+        q_in[offset] = send(q_hbm, qraw.at[dp], S_Q + offset - 1, S_Q + offset - 1, offset)
+    for offset in (2, 3, 1):
+        tab_in[offset] = send(tab_hbm, tabs.at[dp], S_TAB + offset - 1, S_TAB + offset - 1, offset)
+        held_in[offset] = send(held_hbm, helds.at[dp], S_HELD + offset - 1, S_HELD + offset - 1, offset)
+    for number in (L_TAB, L_HELD, L_Q, L_POOL):
+        loads[number].wait()
+    run_block(0, 0, keep_n, keep_ml)
+    know(0)
+    fetch_block(1)
+    run_block(1, 0, send_n, send_ml)
+    pair_in = [send_pair(0)]
+    know(1)
     for number in (L_IDS, L_WEIGHTS, L_RES, L_MGAIN, L_AGAIN):
         loads[number].wait()
     combine_rows(ids, weights, comown, block, slots)
@@ -265,30 +286,19 @@
     for k in range(NDP):
         resblk[k] = resraw[:, width * k : width * k + width]
     resall[block] = resblk[dp]
-    for number in (L_TAB, L_HELD, L_Q, L_POOL):
-        loads[number].wait()
-    run_block(0, 0, keep_n, keep_ml)
-
-    pl.semaphore_wait(barrier, count + 2)
-    for offset in (2, 1):
-        q_in[offset] = send(q_hbm, qraw.at[dp], S_Q + offset - 1, S_Q + offset - 1, offset)
-    for offset in (2, 3, 1):
-        tab_in[offset] = send(tab_hbm, tabs.at[dp], S_TAB + offset - 1, S_TAB + offset - 1, offset)
-        held_in[offset] = send(held_hbm, helds.at[dp], S_HELD + offset - 1, S_HELD + offset - 1, offset)
+    fetch_block(2)
+    cross = group_peer(z, c, 2)
+    q_in[3] = send(qraw.at[cross], qraw.at[cross], S_Q + 2, S_Q + 2, 1)
     for offset in (2, 3, 1):
         peer = group_peer(z, c, offset)
         res_in[offset] = send(resblk.at[peer], resall.at[block], S_RES + offset - 1, S_RES + offset - 1, offset)
         com_in[offset] = send(comown, comall.at[block], S_COM + offset - 1, S_COM + offset - 1, offset)
-    fetch_block(1)
-    run_block(1, 0, send_n, send_ml)
-    pair_in = [send_pair(0)]
-    fetch_block(2)
-    cross = group_peer(z, c, 2)
-    q_in[3] = send(qraw.at[cross], qraw.at[cross], S_Q + 2, S_Q + 2, 1)
     cross_in = [merge_pair(0, pair_in[0])]
+    know(2)
     fetch_block(3)
     run_block(3, 1, send_n, send_ml)
     pair_in.append(send_pair(1))
+    know(3)
     run_block(2, 1, keep_n, keep_ml)
     cross_in.append(merge_pair(1, pair_in[1]))
     xs_ml[...] = keep_ml[0] + keep_ml[1]
@@ -315,13 +325,18 @@
     for pair in range(HEADS // 2):
         lhs[c, :, PAIR * pair : PAIR * pair + PAIR] = att[pl.ds(pair, 2 * ROWS, stride=HEADS // 2), :].astype(BF16)
     lhs_in = send(lhs.at[c], lhs.at[c], S_LHS, S_LHS, 1)
+    for digit in range(4, digits):
+        know(digit)
+    for offset in (1, 2, 3):
+        res_in[offset].wait_recv()
+        com_in[offset].wait_recv()
+    residual = jnp.concatenate([resall[d].astype(F32) for d in range(NDP)], axis=0)
+    share = jnp.concatenate([comall[d] for d in range(NDP)], axis=0)
+    picks = (share > 0).astype(F32).T.astype(BF16)
     loads[L_OW].wait()
     lhs_in.wait_recv()
     rows = jnp.concatenate([lhs[0], lhs[1]], axis=0)
     projected = lax.dot_general(rows, ow[...], (((1,), (1,)), ((), ())), preferred_element_type=F32)
-    for offset in (1, 2, 3):
-        res_in[offset].wait_recv()
-    residual = jnp.concatenate([resall[d].astype(F32) for d in range(NDP)], axis=0)
     stream[z] = (residual + projected.astype(BF16).astype(F32)).astype(BF16)
     stream_in = send(stream.at[z], stream.at[z], S_STREAM, S_STREAM, 2)
     own = stream[z].astype(F32)
@@ -336,10 +351,6 @@
     sum_in = [
         send(sums.at[dp], sums.at[dp], S_SUM + offset - 1, S_SUM + offset - 1, offset) for offset in (2, 3, 1)
     ]
-    for offset in (1, 2, 3):
-        com_in[offset].wait_recv()
-    share = jnp.concatenate([comall[d] for d in range(NDP)], axis=0)
-    picks = (share > 0).astype(F32).T.astype(BF16)
     for copy in sum_in:
         copy.wait_recv()
     square = (sums[0] + sums[1] + sums[2] + sums[3])[:1]
@@ -584,6 +595,7 @@
             dma((count,)),
             dma((2, count)),
             dma((2, count)),
+            pltpu.SemaphoreType.REGULAR((count.bit_length() - 1,)),
         ],
         compiler_params=pltpu.CompilerParams(collective_id=0, has_side_effects=True, vmem_limit_bytes=44 * 2**20),
         name="layer",

time: 74.7 us -> 76.1 us (1.019)
  Pallas kernels: 72.6 us -> 74 us
    pallas_call x1, Pallas kernels: 72.6 us -> 74 us  [layer_call(): pl.pallas_call(layer_kernel, out_shape=(jax.ShapeDtypeStruct((ROWS, NDP *...]
where the time goes in v6:
time: 76.1 us; the launch traced here: 75.9 us
  Pallas kernels  74 us (97%)
  local copies, waits for them, and re-layouts  1.26 us (2%)
    pallas_call x1, Pallas kernels, layer_call(): pl.pallas_call(layer_kernel, out_shape=(jax.ShapeDtypeStruct((ROWS, NDP *...  74 us

profile of v6, /device:TPU:1, one launch (start us, length us, event | category | flops | bytes accessed | tf_op | source)
XLA Modules:
  0.0 75.9 jit_solution(3803033215849470271)
XLA Ops:
  0.6 74.0 %layer.1 = (bf16[8,2880]{1,0:T(8,128)(2,1)S(1)}, bf16[8,5120]{1,0:T(8,128)(2,1)S(1)}) custom-call(bf16[8,4096]{1,0:T(8,128)(2,1)} %q_hbm.1, bf16[128,16,1024]{2,1,0:T(8,128)(2,1)} %pool_hbm.1, s32[8,4,16]{2,1,0:T(4,128)} %tab_hbm.1, s32[4,8]{1,0:T(4,128)} %bitcast.18, f32[1,64]{1,0:T(1,128)} %bitcast.21, bf16[8,2880]{1,0:T(8,128)(2,1)} %res_hbm.1, ...), custom_call_target="tpu_custom_call" | custom-call | tf_op jit(solution)/shard_map/layer/pallas_call | solution.py:531
  74.7 0.6 copy.19
  75.3 0.6 copy.20

commit v7 on v6

--- a/solution.py
+++ b/solution.py
@@ -142,7 +142,7 @@
         taken = taken + hit
 
 
-STEP = 4
+STEP = 8
 
 
 def layer_kernel(
@@ -173,8 +173,10 @@
         pl.semaphore_signal(barrier, inc=1, device_id=neighbour(digit), device_id_type=MESH)
 
     def know(digit):
-        pl.semaphore_signal(round_sem.at[digit], inc=1, device_id=neighbour(digit), device_id_type=MESH)
-        pl.semaphore_wait(round_sem.at[digit], 1)
+        if digit > 0:
+            pl.semaphore_wait(round_sem.at[digit - 1], 1)
+        if digit < digits:
+            pl.semaphore_signal(round_sem.at[digit], inc=1, device_id=neighbour(digit), device_id_type=MESH)
 
     loads = {}
     for number, src, dst in (
@@ -262,19 +264,12 @@
         return send(xs_n.at[number], xr_n.at[1 - number], S_X_N + number, S_X_N + 1 - number, 2)
 
     pl.semaphore_wait(barrier, 3 + digits)
+    know(0)
     for offset in (2, 1):
         q_in[offset] = send(q_hbm, qraw.at[dp], S_Q + offset - 1, S_Q + offset - 1, offset)
     for offset in (2, 3, 1):
         tab_in[offset] = send(tab_hbm, tabs.at[dp], S_TAB + offset - 1, S_TAB + offset - 1, offset)
         held_in[offset] = send(held_hbm, helds.at[dp], S_HELD + offset - 1, S_HELD + offset - 1, offset)
-    for number in (L_TAB, L_HELD, L_Q, L_POOL):
-        loads[number].wait()
-    run_block(0, 0, keep_n, keep_ml)
-    know(0)
-    fetch_block(1)
-    run_block(1, 0, send_n, send_ml)
-    pair_in = [send_pair(0)]
-    know(1)
     for number in (L_IDS, L_WEIGHTS, L_RES, L_MGAIN, L_AGAIN):
         loads[number].wait()
     combine_rows(ids, weights, comown, block, slots)
@@ -286,6 +281,13 @@
     for k in range(NDP):
         resblk[k] = resraw[:, width * k : width * k + width]
     resall[block] = resblk[dp]
+    for number in (L_TAB, L_HELD, L_Q, L_POOL):
+        loads[number].wait()
+    run_block(0, 0, keep_n, keep_ml)
+    fetch_block(1)
+    run_block(1, 0, send_n, send_ml)
+    pair_in = [send_pair(0)]
+    know(1)
     fetch_block(2)
     cross = group_peer(z, c, 2)
     q_in[3] = send(qraw.at[cross], qraw.at[cross], S_Q + 2, S_Q + 2, 1)
@@ -439,6 +441,7 @@
             rbuf[j, first_place : first_place + batch] = total.reshape(batch, slots, width)
             each(max(first_place, 1), first_place + batch, lambda place: giveback(j, place).start())
 
+    know(digits)
     each(1, count, lambda place: dispatch(place).start())
     for j in range(2):
         arr[c, j, 0] = outbox[j, expert]

time: 76.1 us -> 71.7 us (0.942)
  Pallas kernels: 74 us -> 69.7 us
    pallas_call x1, Pallas kernels: 74 us -> 69.7 us  [layer_call(): pl.pallas_call(layer_kernel, out_shape=(jax.ShapeDtypeStruct((ROWS, NDP *...]
where the time goes in v7:
time: 71.7 us; the launch traced here: 71.6 us
  Pallas kernels  69.7 us (97%)
  local copies, waits for them, and re-layouts  1.26 us (2%)
    pallas_call x1, Pallas kernels, layer_call(): pl.pallas_call(layer_kernel, out_shape=(jax.ShapeDtypeStruct((ROWS, NDP *...  69.7 us

profile of v7, /device:TPU:1, one launch (start us, length us, event | category | flops | bytes accessed | tf_op | source)
XLA Modules:
  0.0 71.6 jit_solution(14380567536993579143)
XLA Ops:
  0.6 69.7 %layer.1 = (bf16[8,2880]{1,0:T(8,128)(2,1)S(1)}, bf16[8,5120]{1,0:T(8,128)(2,1)S(1)}) custom-call(bf16[8,4096]{1,0:T(8,128)(2,1)} %q_hbm.1, bf16[128,16,1024]{2,1,0:T(8,128)(2,1)} %pool_hbm.1, s32[8,4,16]{2,1,0:T(4,128)} %tab_hbm.1, s32[4,8]{1,0:T(4,128)} %bitcast.18, f32[1,64]{1,0:T(1,128)} %bitcast.21, bf16[8,2880]{1,0:T(8,128)(2,1)} %res_hbm.1, ...), custom_call_target="tpu_custom_call" | custom-call | tf_op jit(solution)/shard_map/layer/pallas_call | solution.py:534
  70.3 0.6 copy.19
  70.9 0.6 copy.20

commit v8 on v7

--- a/solution.py
+++ b/solution.py
@@ -27,7 +27,8 @@
 
 S_TAB, S_HELD, S_Q, S_RES, S_COM, S_SUM, S_QKV = range(0, 21, 3)
 S_PAIR_N, S_PAIR_ML, S_X_N, S_PART, S_NEXT = range(21, 31, 2)
-S_X_ML, S_LHS, S_STREAM, S_OUT, N_SEM = 31, 32, 33, 34, 38
+BATCHES = 4
+S_X_ML, S_LHS, S_STREAM, S_OUT, N_SEM = 31, 32, 33, 34, 34 + 2 * BATCHES
 L_TAB, L_HELD, L_Q, L_POOL, L_SINK, L_IDS, L_WEIGHTS, L_RES, L_OW, L_MGAIN, L_GATE, L_UP, L_DOWN, L_AGAIN, L_QKV = range(15)
 
 
@@ -395,7 +396,7 @@
 
         lax.fori_loop(first, last, step, 0)
 
-    batch = count // 2
+    batch = count // BATCHES
     batch_rows = batch * slots
 
     def pass_on(place):
@@ -446,14 +447,15 @@
     for j in range(2):
         arr[c, j, 0] = outbox[j, expert]
     forward(0).start()
-    each(1, batch, pass_on)
     for number in (L_GATE, L_UP, L_DOWN):
         loads[number].wait()
-    incoming = apply_experts(0)
-    each(batch, count, pass_on)
-    give_back(0, incoming)
-    incoming = apply_experts(1)
-    give_back(1, incoming)
+    incoming = None
+    for number in range(BATCHES):
+        each(max(1, batch * number), batch * (number + 1), pass_on)
+        if number > 0:
+            give_back(number - 1, incoming)
+        incoming = apply_experts(number)
+    give_back(BATCHES - 1, incoming)
     for j in range(2):
         ret[j, expert] = rbuf[j, 0]
 
@@ -577,11 +579,11 @@
             vmem((NDP, 8, 128), F32),
             vmem((2, count, slots, width), BF16),
             vmem((2, 2, count, slots, width), BF16),
-            vmem((all_slots // 2, hidden), F32),
-            vmem((all_slots // 2, hidden), F32),
-            vmem((2, 2, all_slots // 2, width), BF16),
-            vmem((2, 2, all_slots // 2, width), BF16),
-            vmem((2, all_slots // 2, width), F32),
+            vmem((all_slots // BATCHES, hidden), F32),
+            vmem((all_slots // BATCHES, hidden), F32),
+            vmem((BATCHES, 2, all_slots // BATCHES, width), BF16),
+            vmem((BATCHES, 2, all_slots // BATCHES, width), BF16),
+            vmem((2, all_slots // BATCHES, width), F32),
             vmem((2, count, slots, width), BF16),
             vmem((2, count, slots, width), BF16),
             vmem((2, group_rows, width), BF16),

time: 71.7 us -> 70.9 us (0.989)
  Pallas kernels: 69.7 us -> 68.9 us
    pallas_call x1, Pallas kernels: 69.7 us -> 68.9 us  [layer_call(): pl.pallas_call(layer_kernel, out_shape=(jax.ShapeDtypeStruct((ROWS, NDP *...]
where the time goes in v8:
time: 70.9 us; the launch traced here: 70.8 us
  Pallas kernels  68.9 us (97%)
  local copies, waits for them, and re-layouts  1.26 us (2%)
    pallas_call x1, Pallas kernels, layer_call(): pl.pallas_call(layer_kernel, out_shape=(jax.ShapeDtypeStruct((ROWS, NDP *...  68.9 us

profile of v8, /device:TPU:1, one launch (start us, length us, event | category | flops | bytes accessed | tf_op | source)
XLA Modules:
  0.0 70.8 jit_solution(9130018910192996771)
XLA Ops:
  0.6 68.9 %layer.1 = (bf16[8,2880]{1,0:T(8,128)(2,1)S(1)}, bf16[8,5120]{1,0:T(8,128)(2,1)S(1)}) custom-call(bf16[8,4096]{1,0:T(8,128)(2,1)} %q_hbm.1, bf16[128,16,1024]{2,1,0:T(8,128)(2,1)} %pool_hbm.1, s32[8,4,16]{2,1,0:T(4,128)} %tab_hbm.1, s32[4,8]{1,0:T(4,128)} %bitcast.18, f32[1,64]{1,0:T(1,128)} %bitcast.21, bf16[8,2880]{1,0:T(8,128)(2,1)} %res_hbm.1, ...), custom_call_target="tpu_custom_call" | custom-call | tf_op jit(solution)/shard_map/layer/pallas_call | solution.py:536
  69.5 0.6 copy.19
  70.1 0.6 copy.20

commit v9 on v8

--- a/solution.py
+++ b/solution.py
@@ -247,6 +247,8 @@
         half = z if number == 0 else 1 - z
         return pltpu.roll(tile, lax.rem(PAIR - half * ROWS, PAIR), 1)
 
+    cross_ml = []
+
     def merge_pair(number, incoming):
         for copy in incoming:
             copy.wait_recv()
@@ -255,6 +257,9 @@
         left, right = jnp.exp(mine - high), jnp.exp(other - high)
         total = mine * pltpu.roll(left, HD, 1) + other * pltpu.roll(right, HD, 1)
         keep_ml[number] = jnp.where(lane < HD, high, total)
+        if number == 1:
+            xs_ml[...] = keep_ml[0] + keep_ml[1]
+            cross_ml.append(send(xs_ml, xr_ml, S_X_ML, S_X_ML, 2))
         left, right = factors(left, number), factors(right, number)
         for row in range(ROWS):
             merged = keep_n[number, row] * pair_columns(left[:, row : row + 1]) + recv_n[number, row].astype(
@@ -304,10 +309,7 @@
     know(3)
     run_block(2, 1, keep_n, keep_ml)
     cross_in.append(merge_pair(1, pair_in[1]))
-    xs_ml[...] = keep_ml[0] + keep_ml[1]
-    cross_ml = send(xs_ml, xr_ml, S_X_ML, S_X_ML, 2)
-
-    cross_ml.wait_recv()
+    cross_ml[0].wait_recv()
     loads[L_SINK].wait()
     mine, other, sink = xs_ml[...], xr_ml[...], sink_columns(sinks[...])
     top = jnp.maximum(jnp.maximum(mine, other), sink)
@@ -315,7 +317,7 @@
     total = mine * pltpu.roll(left, HD, 1) + other * pltpu.roll(right, HD, 1)
     below = pltpu.roll(total, HD, 1) + jnp.exp(sink - top)
     left, right = left / below, right / below
-    for number in (0, 1):
+    for number in (1, 0):
         cross_in[1 - number].wait_recv()
         one, two = factors(left, number), factors(right, number)
         half = z if number == 0 else 1 - z

time: 70.9 us -> 70.1 us (0.989)
  Pallas kernels: 68.9 us -> 68.1 us
    pallas_call x1, Pallas kernels: 68.9 us -> 68.1 us  [layer_call(): pl.pallas_call(layer_kernel, out_shape=(jax.ShapeDtypeStruct((ROWS, NDP *...]
where the time goes in v9:
time: 70.1 us; the launch traced here: 70 us
  Pallas kernels  68.1 us (97%)
  local copies, waits for them, and re-layouts  1.26 us (2%)
    pallas_call x1, Pallas kernels, layer_call(): pl.pallas_call(layer_kernel, out_shape=(jax.ShapeDtypeStruct((ROWS, NDP *...  68.1 us

profile of v9, /device:TPU:1, one launch (start us, length us, event | category | flops | bytes accessed | tf_op | source)
XLA Modules:
  0.0 70.0 jit_solution(18301172521313370255)
XLA Ops:
  0.6 68.1 %layer.1 = (bf16[8,2880]{1,0:T(8,128)(2,1)S(1)}, bf16[8,5120]{1,0:T(8,128)(2,1)S(1)}) custom-call(bf16[8,4096]{1,0:T(8,128)(2,1)} %q_hbm.1, bf16[128,16,1024]{2,1,0:T(8,128)(2,1)} %pool_hbm.1, s32[8,4,16]{2,1,0:T(4,128)} %tab_hbm.1, s32[4,8]{1,0:T(4,128)} %bitcast.18, f32[1,64]{1,0:T(1,128)} %bitcast.21, bf16[8,2880]{1,0:T(8,128)(2,1)} %res_hbm.1, ...), custom_call_target="tpu_custom_call" | custom-call | tf_op jit(solution)/shard_map/layer/pallas_call | solution.py:538
  68.8 0.6 copy.19
  69.4 0.6 copy.20
